TPU v7x, 128 devices: a whole 4x4x4 slice. The times are simulated.
128 devices in a mesh: tm: 16 (over x, y), tile: 8 (over z, core).
Axes of the slice: x: 4, y: 4, z: 4, core: 2. Of those that a mesh axis runs over, the one named last changes fastest.
Arguments:
- observed: float32 [9, 64, 8192], P(None, 'tile', 'tm'), may hold values from -6 to 6
- increments: float32 [9, 64, 8192], P(None, 'tile', 'tm'), may hold values from -0.15625 to 0.15625
- model: float32 [512, 256], P(('tm', 'tile')), may hold values from -6 to 6
- kernel: bfloat16 [256, 4, 9, 256, 256], P(('tm', 'tile')), may hold values from -0.1875 to 0.1875
- tile_index: int32 [256, 4], P(('tm', 'tile')), may hold values from 0 to 511, all different within a row
- station_of: int32 [64, 8192], P('tile', 'tm'), may hold values from 0 to 65535, as said below
- line_length: int32 [64], P('tile'), may hold values from 2048 to 8192, as said below
Outputs:
- grad_model: float32 [512, 256], P(('tm', 'tile'))
- grad_increments: float32 [9, 64, 8192], P(None, 'tile', 'tm')
Inputs may be any that keep to these rules, and one draw needn't show every extreme that they name: `station_of`: in the samples of one index pair of tile and tm (its block of lines and block of time), no station tile (value // 256) holds more than 32 samples, and one holds exactly 32. `line_length`: some line has all 8192 samples. `tile_index`: each row names 4 different cell tiles, and every cell tile is named by some row.
All inputs are finite; a program needn't handle non-finite values.
Results may differ from a plain program's by a relative error of at most 0.0031.
Values may be sent and summed in bfloat16 or wider, within the bound.
A program may use at most 128 MiB of HBM per device.

v0:
```python
import math

import jax
import jax.numpy as jnp
from jax import lax
from jax.sharding import PartitionSpec as P


def prefix(part, axis, combine, identity, reverse):
    count = lax.axis_size(axis)
    place = lax.axis_index(axis)
    ahead = count - 1 - place if reverse else place
    gathered = lax.all_gather(part, axis)
    state = jnp.zeros_like(part) + jnp.asarray(identity, part.dtype)

    def one(turn, state):
        source = count - 1 - turn if reverse else turn
        return combine(state, lax.dynamic_index_in_dim(gathered, source, 0, False))

    return lax.fori_loop(0, ahead, one, state)


def running_sum(values, backward):
    components, line_count, step_count = values.shape
    block_size = 128
    pieces = values.reshape(components, line_count, step_count // block_size, block_size)
    rows_index = lax.broadcasted_iota(jnp.int32, (block_size, block_size), 0)
    cols_index = lax.broadcasted_iota(jnp.int32, (block_size, block_size), 1)
    if backward:
        triangle = (rows_index >= cols_index).astype(jnp.float32)
    else:
        triangle = (rows_index <= cols_index).astype(jnp.float32)
    within = jnp.matmul(pieces, triangle, precision=lax.Precision.HIGHEST)
    if backward:
        block_total = within[..., 0]
        offsets = jnp.flip(jnp.cumsum(jnp.flip(block_total, 2), axis=2), 2) - block_total
    else:
        block_total = within[..., -1]
        offsets = jnp.cumsum(block_total, axis=2) - block_total
    return (within + offsets[..., None]).reshape(values.shape)


def shards(observed, increments, model, kernel, tile_index, station_of, line_length):
    components, line_count, step_count = observed.shape
    tiles_here = kernel.shape[0]
    tile_width = kernel.shape[-1]
    time_devices = lax.axis_size("tm")
    device_count = time_devices * lax.axis_size("tile")
    station_count = tiles_here * device_count
    row_count = line_count * step_count
    capacity = 2 * row_count // station_count
    total_steps = step_count * time_devices
    line_total = line_count * lax.axis_size("tile")
    station_gain = 1.0 / math.sqrt(line_total * total_steps / (station_count * tile_width))
    own_index = lax.axis_index("tm")
    partial_walk = running_sum(increments, False)
    walk_totals = partial_walk[:, :, -1]
    earlier = prefix(walk_totals, "tm", jnp.add, jnp.zeros_like(walk_totals), False)
    drift_walk = partial_walk + earlier[:, :, None]
    positions = own_index * step_count + jnp.arange(step_count, dtype=jnp.int32)
    inside = positions[None, :] < line_length[:, None]
    offset = drift_walk - observed
    flat_station = station_of.reshape(row_count)
    flat_inside = inside.reshape(row_count)
    flat_offset = offset.reshape(components, row_count)
    whole_model = lax.all_gather(model.astype(jnp.bfloat16), ("tm", "tile"), axis=0, tiled=True)
    chosen = whole_model[tile_index]
    predicted = jnp.einsum("skcij,skj->csi", kernel, chosen, preferred_element_type=jnp.float32)
    tile_of_row = flat_station // tile_width
    inner_station = jnp.where(flat_inside, flat_station % tile_width, tile_width)
    ordering = jnp.argsort(tile_of_row, stable=True)
    sorted_tiles = tile_of_row[ordering]
    starts = jnp.searchsorted(sorted_tiles, jnp.arange(station_count, dtype=jnp.int32))
    placed = jnp.arange(row_count, dtype=jnp.int32) - starts[sorted_tiles]
    slot_sorted = sorted_tiles * capacity + placed
    slot_of_row = jnp.zeros((row_count,), jnp.int32).at[ordering].set(slot_sorted)
    outgoing = (
        jnp.zeros((components, station_count * capacity), jnp.float32)
        .at[:, slot_of_row]
        .set(flat_offset)
    )
    labels = (
        jnp.full((station_count * capacity,), tile_width, jnp.int32)
        .at[slot_of_row]
        .set(inner_station)
    )
    arrived, arrived_labels = (
        lax.all_to_all(
            outgoing.reshape(components, station_count, capacity),
            ("tm", "tile"),
            split_axis=1,
            concat_axis=2,
            tiled=True,
        ),
        lax.all_to_all(
            labels.reshape(1, station_count, capacity),
            ("tm", "tile"),
            split_axis=1,
            concat_axis=2,
            tiled=True,
        ),
    )
    occupied = arrived_labels < tile_width
    station_ids = jnp.arange(tile_width, dtype=jnp.int32)
    matches = (arrived_labels[0][:, :, None] == station_ids).astype(jnp.float32)
    picked = jnp.einsum("csi,sri->csr", predicted, matches, precision=lax.Precision.HIGHEST)
    answer = jnp.where(occupied, picked + arrived, 0.0)
    station_sums = jnp.einsum("csr,sri->csi", answer, matches, precision=lax.Precision.HIGHEST)
    station_half = (station_sums * station_gain).astype(jnp.bfloat16)
    returned = lax.all_to_all(
        answer.astype(jnp.bfloat16), ("tm", "tile"), split_axis=2, concat_axis=1, tiled=True
    ).astype(answer.dtype)
    residual = returned.reshape(components, station_count * capacity)[:, slot_of_row]
    contributions = jnp.einsum(
        "skcij,csi->skj", kernel, station_half, preferred_element_type=jnp.float32
    )
    cell_total = model.shape[0] * device_count
    local_grad = (
        jnp.zeros((cell_total, tile_width), jnp.float32)
        .at[tile_index.reshape(-1)]
        .add(contributions.reshape(-1, tile_width))
    )
    grad_model = lax.psum_scatter(local_grad, ("tm", "tile"), scatter_dimension=0, tiled=True)
    residual_block = residual.reshape(components, line_count, step_count)
    partial_tail = running_sum(residual_block, True)
    tail_totals = partial_tail[:, :, 0]
    remaining = prefix(tail_totals, "tm", jnp.add, jnp.zeros_like(tail_totals), True)
    grad_increments = (partial_tail + remaining[:, :, None]) / math.sqrt(total_steps)
    return (grad_model, grad_increments)


def solution(mesh):
    in_specs = (
        P(None, "tile", "tm"),
        P(None, "tile", "tm"),
        P(("tm", "tile"), None),
        P(("tm", "tile"), None, None, None, None),
        P(("tm", "tile"), None),
        P("tile", "tm"),
        P("tile"),
    )
    out_specs = (P(("tm", "tile"), None), P(None, "tile", "tm"))
    return jax.shard_map(shards, mesh=mesh, in_specs=in_specs, out_specs=out_specs, check_vma=False)
```

profile of v0, /device:TPU:1, one launch (start us, length us, event | category | flops | bytes accessed | tf_op | source)
XLA Modules:
  0.0 415.5 jit_solution(10348112344737669025)
XLA Ops:
  7.2 0.8 compare_bitcast_fusion
  8.0 0.7 copy.127
  8.7 5.8 %sort.17 = (s32[4096]{0:T(1024)}, s32[4096]{0:T(1024)S(1)}) sort(s32[4096]{0:T(1024)S(1)} %get-tuple-element.237, s32[4096]{0:T(1024)S(1)} %iota.37), dimensions={0}, to_apply=%region_0.0 | sort | flops 49152 | bytes 65536 | tf_op jit(solution)/shard_map/jit(argsort)/sort | solution.py:71
  14.5 23.0 %gather_fusion.1 = s32[4096]{0:T(1024)S(1)} fusion(s32[4096]{0:T(1024)S(1)} %get-tuple-element.237, s32[4096]{0:T(1024)S(1)} %get-tuple-element.238), kind=kCustom, calls=%fused_computation.1 | custom fusion | bytes 49152 | tf_op jit(solution)/shard_map/gather | solution.py:72
  37.6 23.3 %while.48 = (s32[]{:T(128)}, u32[256]{0:T(256)S(1)}, u32[256]{0:T(256)S(1)}, s32[4096]{0:T(1024)S(1)}, s32[]{:T(128)}, /*index=5*/s32[]{:T(128)}, s32[]{}) while((s32[]{:T(128)}, u32[256]{0:T(256)S(1)}, u32[256]{0:T(256)S(1)}, s32[4096]{0:T(1024)S(1)}, s32[]{:T(128)}, /*index=5*/s32[]{:T(128)}, s32[]{}) %tuple.85), condition=%wide.region_2.3_spmd.clone, body=%wide.region_1.2_spmd.clone.sunk | while | flops 4356 | bytes 16484 | solution.py:73
  37.6 1.7 gather_fusion
  39.4 1.7 gather_fusion
  41.2 1.7 gather_fusion
  43.0 1.7 gather_fusion
  44.8 1.7 gather_fusion
  46.6 1.7 gather_fusion
  48.4 1.7 gather_fusion
  50.2 1.7 gather_fusion
  52.0 1.7 gather_fusion
  53.8 1.7 gather_fusion
  55.6 1.7 gather_fusion
  57.3 1.7 gather_fusion
  59.1 1.7 gather_fusion
  60.9 25.7 %gather_fusion.2 = s32[4096]{0:T(1024)S(1)} fusion(s32[256]{0:T(256)S(1)} %convert_element_type.26, s32[4096]{0:T(1024)S(1)} %broadcast_clamp_fusion.1), kind=kCustom, calls=%fused_computation.2 | custom fusion | bytes 49152 | tf_op jit(solution)/shard_map/gather | solution.py:74
  86.7 15.5 %scatter_custom_fusion = s32[4096]{0:T(1024)S(1)} fusion(s32[4096]{0:T(1024)S(1)} %get-tuple-element.239, s32[4096]{0:T(1024)S(1)} %subtract_add_fusion, s32[]{:T(128)} %constant.112.clone.1), kind=kCustom, calls=%fused_computation.77 | custom fusion | bytes 16388 | tf_op jit(solution)/shard_map/scatter | solution.py:76
  102.3 15.5 %scatter_custom_fusion.1 = s32[8192]{0:T(1024)S(1)} fusion(s32[4096]{0:T(1024)S(1)} %get-tuple-element.235, s32[4096]{0:T(1024)S(1)} %get-tuple-element.236, s32[]{:T(128)} %constant.114.clone.1), kind=kCustom, calls=%fused_computation.67 | custom fusion | bytes 32772 | tf_op jit(solution)/shard_map/scatter | solution.py:85
  117.8 0.7 reshape.102
  118.6 11.5 %all-to-all-start = ((s32[1,256,32]{2,0,1:T(1,128)}), s32[1,256,32]{2,0,1:T(1,128)S(1)}, u32[]{:S(2)}, u32[]{:S(2)}) async-start(s32[1,256,32]{2,0,1:T(1,128)} %bitcast.5), calls=%async_computation | async-start | bytes 262144 | tf_op jit(solution)/shard_map/all_to_all | solution.py:95
  130.2 0.3 convolution_bitcast_fusion
  130.5 0.7 reduce-window_subtract_fusion
  131.2 0.3 copy.91
  131.5 0.1 broadcast_add_fusion.1
  132.0 18.4 %all-gather = f32[144,8,1]{1,2,0:T(1,128)S(1)} all-gather(f32[9,8,1]{1,2,0:T(1,128)S(1)} %copy.94), channel_id=2, replica_groups=mesh['tm'=16,'tile'=8] {'tm'}, dimensions={0}, use_global_device_ids=true | all-gather | bytes 4896 | tf_op jit(solution)/shard_map/all_gather | solution.py:13
  150.6 42.2 %all-gather.2 = bf16[128,4,256]{2,1,0:T(4,128)(2,1)S(1)} all-gather(bf16[1,4,256]{2,1,0:T(4,128)(2,1)S(1)} %convert_bitcast_fusion), channel_id=1, replica_groups=mesh['tm'=16,'tile'=8] {'tm','tile'}, dimensions={0}, use_global_device_ids=true | all-gather | bytes 264192 | tf_op jit(solution)/shard_map/all_gather | solution.py:66
  193.0 0.6 gather_fusion.3
  193.7 6.2 %convolution_bitcast_fusion.1 = f32[2,1,9,256,1]{3,1,4,2,0:T(1,128)S(1)} fusion(bf16[2,4,9,256,256]{4,3,2,1,0:T(8,128)(2,1)} %param.16, bf16[2,4,256,1,1]{2,3,1,4,0:T(2,128)(2,1)S(1)} %reshape.204), kind=kOutput, calls=%fused_computation.30 | convolution fusion | flops 9437184 | bytes 9459712 | tf_op jit(solution)/shard_map/skcij,skj->csi/dot_general | solution.py:68
  199.9 0.7 copy.122
  200.6 12.8 %scatter_custom_fusion.2 = f32[9,8192]{0,1:T(8,128)} fusion(s32[4096]{0:T(1024)S(1)} %get-tuple-element.235, f32[4096,9]{1,0:T(8,128)S(1)} %bitcast.115, f32[]{:T(128)} %constant.111.clone.1), kind=kCustom, calls=%fused_computation.24 | custom fusion | bytes 294916 | tf_op jit(solution)/shard_map/scatter | solution.py:80
  213.3 3.3 copy.99
  216.6 1.4 reshape.213
  218.1 4.7 %all-to-all-start.1 = ((f32[128,1,576]{2,1,0:T(1,128)}), f32[128,1,576]{2,1,0:T(1,128)S(1)}, u32[]{:S(2)}, u32[]{:S(2)}) async-start(f32[128,1,576]{2,1,0:T(1,128)} %reshape.213), calls=%async_computation.1 | async-start | bytes 655360 | tf_op jit(solution)/shard_map/all_to_all | solution.py:88
  222.9 3.9 fusion.5
  226.8 7.5 %all-to-all-done.1 = f32[128,1,576]{2,1,0:T(1,128)S(1)} async-done(((f32[128,1,576]{2,1,0:T(1,128)}), f32[128,1,576]{2,1,0:T(1,128)S(1)}, u32[]{:S(2)}, u32[]{:S(2)}) %all-to-all-start.1) | async-done | bytes 294944 | tf_op jit(solution)/shard_map/all_to_all | solution.py:88
  234.3 0.5 broadcast.166
  234.8 1.4 reduce
  236.2 0.6 reshape.214
  236.8 0.4 copy.100
  237.2 0.1 copy.101
  237.3 0.6 all_to_all.41
  238.0 0.4 fusion.37
  238.3 2.8 copy.103
  241.2 4.8 %reshape.215 = bf16[128,2,288]{2,1,0:T(2,128)(2,1)} reshape(bf16[4096,2,9]{2,1,0:T(2,128)(2,1)S(1)} %bitcast.110) | data formatting | bytes 294912
  246.0 4.7 %all-to-all-start.2 = ((bf16[128,2,288]{2,1,0:T(2,128)(2,1)}), bf16[128,2,288]{2,1,0:T(2,128)(2,1)S(1)}, u32[]{:S(2)}, u32[]{:S(2)}) async-start(bf16[128,2,288]{2,1,0:T(2,128)(2,1)} %reshape.215), calls=%async_computation.2 | async-start | bytes 393216 | tf_op jit(solution)/shard_map/all_to_all | solution.py:110
  250.6 0.3 all-reduce.3.cloned.1.call-start
  250.9 3.0 fusion.12
  253.9 5.0 %fusion.26 = f32[2,1,4,256,1]{3,1,4,2,0:T(1,128)S(1)} fusion(bf16[2,4,9,256,256]{4,3,2,1,0:T(8,128)(2,1)} %param.16, bf16[9,2,256,1,1]{2,0,1,3,4:T(8,128)(2,1)S(1)} %fusion.12), kind=kOutput, calls=%fused_computation.60 | convolution fusion | flops 9437184 | bytes 9454592 | tf_op jit(solution)/shard_map/skcij,csi->skj/dot_general | solution.py:114
  258.9 1.4 scatter_custom_fusion.3
  260.4 0.6 all-to-all-done.2
  260.9 4.9 %reshape.216 = bf16[4096,2,9]{2,1,0:T(2,128)(2,1)S(1)} reshape(bf16[128,2,288]{2,1,0:T(2,128)(2,1)S(1)} %all-to-all-done.2) | data formatting | bytes 294912
  265.8 1.9 copy.124
  267.7 12.9 %gather_fusion.4 = bf16[4096,9]{1,0:T(8,128)(2,1)S(1)} fusion(bf16[9,8192]{0,1:T(8,128)(2,1)} %bitcast.113, s32[4096]{0:T(1024)S(1)} %get-tuple-element.234), kind=kCustom, calls=%fused_computation.4 | custom fusion | bytes 163840 | tf_op jit(solution)/shard_map/gather | solution.py:113
  280.6 0.4 fusion.22
  281.1 0.3 copy.107
  281.5 0.1 broadcast_add_fusion
  281.9 18.6 %all-gather.1 = f32[144,8,1]{1,2,0:T(1,128)S(1)} all-gather(f32[9,8,1]{1,2,0:T(1,128)S(1)} %copy.110), channel_id=3, replica_groups=mesh['tm'=16,'tile'=8] {'tm'}, dimensions={0}, use_global_device_ids=true | all-gather | bytes 4896 | tf_op jit(solution)/shard_map/all_gather | solution.py:13
  300.7 0.8 while.47
  301.6 0.8 add_multiply_fusion
  302.4 105.0 %all-reduce.3.cloned.1.call-done = f32[512,256]{1,0:T(8,128)} async-done(((f32[512,256]{1,0:T(8,128)}), f32[512,256]{1,0:T(8,128)}) %all-reduce.3.cloned.1.call-update) | async-done | bytes 524304
  407.4 1.3 constant_dynamic-slice_fusion.2
  (125 shorter events, 2.4 us)
Async XLA Ops:
  7.2 123.0 %copy-start = (f32[9,8,512]{2,1,0:T(8,128)S(1)}, f32[9,8,512]{2,1,0:T(8,128)}, u32[]{:S(2)}) copy-start(f32[9,8,512]{2,1,0:T(8,128)} %param.14) | copy-start | bytes 442372
  60.9 69.2 %copy-start.3 = (s32[2,4]{1,0:T(2,128)S(1)}, s32[2,4]{1,0:T(2,128)}, u32[]{:S(2)}) copy-start(s32[2,4]{1,0:T(2,128)} %param.17) | copy-start | bytes 100
  60.9 89.7 %copy-start.2 = (f32[4,256]{1,0:T(4,128)S(1)}, f32[4,256]{1,0:T(4,128)}, u32[]{:S(2)}) copy-start(f32[4,256]{1,0:T(4,128)} %param.15) | copy-start | bytes 12292
  86.7 106.9 %copy-start.1 = (f32[9,8,512]{2,1,0:T(8,128)S(1)}, f32[9,8,512]{2,1,0:T(8,128)}, u32[]{:S(2)}) copy-start(f32[9,8,512]{2,1,0:T(8,128)} %param.13) | copy-start | bytes 442372
  118.6 99.5 %all-to-all-start = ((s32[1,256,32]{2,0,1:T(1,128)}), s32[1,256,32]{2,0,1:T(1,128)S(1)}, u32[]{:S(2)}, u32[]{:S(2)}) async-start(s32[1,256,32]{2,0,1:T(1,128)} %bitcast.5), calls=%async_computation | async-start | bytes 262144 | tf_op jit(solution)/shard_map/all_to_all | solution.py:95
  218.1 16.2 %all-to-all-start.1 = ((f32[128,1,576]{2,1,0:T(1,128)}), f32[128,1,576]{2,1,0:T(1,128)S(1)}, u32[]{:S(2)}, u32[]{:S(2)}) async-start(f32[128,1,576]{2,1,0:T(1,128)} %reshape.213), calls=%async_computation.1 | async-start | bytes 655360 | tf_op jit(solution)/shard_map/all_to_all | solution.py:88
  246.0 15.0 %all-to-all-start.2 = ((bf16[128,2,288]{2,1,0:T(2,128)(2,1)}), bf16[128,2,288]{2,1,0:T(2,128)(2,1)S(1)}, u32[]{:S(2)}, u32[]{:S(2)}) async-start(bf16[128,2,288]{2,1,0:T(2,128)(2,1)} %reshape.215), calls=%async_computation.2 | async-start | bytes 393216 | tf_op jit(solution)/shard_map/all_to_all | solution.py:110
  250.6 156.8 %all-reduce.3.cloned.1.call-start = ((), (), s32[]{:S(2)}) async-start(), calls=%async_computation.3 | async-start | bytes 1048576
Sparse Core Ops, SparseCore 0:
  260.5 146.8 all-reduce.2
where the time goes:
time: 416 us
  local copies, waits for them, and re-layouts  155 us (37%)
  waiting for transfers between devices  113 us (27%)
  blocking collectives  79.2 us (19%)
  starting transfers between devices  21.1 us (5%)
  matrix products  18.8 us (5%)
  between operations  14.5 us (3%)
  other arithmetic  12.3 us (3%)
    unnamed x2, waiting for transfers between devices  105 us
    all_gather x1, blocking collectives, shards(): lax.all_gather(model.astype(jnp.bfloat16), ('tm', 'tile'), axis=0, tiled=...  42.2 us
    all_gather x2, blocking collectives, prefix(): gathered = lax.all_gather(part, axis)  37 us
    gather x1, local copies, waits for them, and re-layouts, shards(): placed = jnp.arange(row_count, dtype=jnp.int32) - starts[sorted_tiles]  25.7 us
    gather x1, local copies, waits for them, and re-layouts, shards(): sorted_tiles = tile_of_row[ordering]  23 us
    gather x13, local copies, waits for them, and re-layouts, shards(): jnp.searchsorted(sorted_tiles, jnp.arange(station_count, dtype=jnp.int32))  22.4 us
    scatter x1, local copies, waits for them, and re-layouts, shards(): labels = jnp.full((station_count * capacity,), tile_width, jnp.int32).at[...  15.5 us
    scatter x1, local copies, waits for them, and re-layouts, shards(): jnp.zeros((row_count,), jnp.int32).at[ordering].set(slot_sorted)  15.5 us
  transfers between devices with their start and end apart: 4, of which 3 were waited for; matrix products, arithmetic and copies ran while one was open for 15% of the time, Pallas kernels for 0%

commit v1 on v0

v1 whole, which is shorter than its diff:
```python
import math

import jax
import jax.numpy as jnp
from jax import lax
from jax.sharding import PartitionSpec as P

BF = jnp.bfloat16
F32 = jnp.float32
AXES = ("tm", "tile")


def parts(x):
    hi = x.astype(BF)
    rest = x - hi.astype(F32)
    mid = rest.astype(BF)
    low = (rest - mid.astype(F32)).astype(BF)
    return hi, mid, low


def running_sum(values, backward):
    components, line_count, step_count = values.shape
    block_size = 128
    pieces = values.reshape(components, line_count, step_count // block_size, block_size)
    rows_index = lax.broadcasted_iota(jnp.int32, (block_size, block_size), 0)
    cols_index = lax.broadcasted_iota(jnp.int32, (block_size, block_size), 1)
    if backward:
        triangle = (rows_index >= cols_index).astype(F32)
    else:
        triangle = (rows_index <= cols_index).astype(F32)
    within = jnp.matmul(pieces, triangle, precision=lax.Precision.HIGHEST)
    count = step_count // block_size
    if backward:
        block_total = within[..., 0]
        carry = [sum([block_total[..., j] for j in range(i + 1, count)], jnp.zeros_like(block_total[..., 0])) for i in range(count)]
    else:
        block_total = within[..., -1]
        carry = [sum([block_total[..., j] for j in range(i)], jnp.zeros_like(block_total[..., 0])) for i in range(count)]
    offsets = jnp.stack(carry, axis=-1)
    return (within + offsets[..., None]).reshape(values.shape)


def swap(x, axes):
    return lax.all_to_all(x, axes, split_axis=0, concat_axis=0, tiled=True)


def beyond(part, backward):
    count = lax.axis_size("tm")
    place = lax.axis_index("tm")
    everyone = swap(jnp.broadcast_to(part[None], (count,) + part.shape), "tm")
    order = jnp.arange(count)
    keep = (order > place) if backward else (order < place)
    return jnp.sum(jnp.where(keep[:, None, None], everyone, 0.0), axis=0)


def shards(observed, increments, model, kernel, tile_index, station_of, line_length):
    components, line_count, step_count = observed.shape
    tiles_here = kernel.shape[0]
    tile_width = kernel.shape[-1]
    time_devices = lax.axis_size("tm")
    device_count = time_devices * lax.axis_size("tile")
    station_count = tiles_here * device_count
    row_count = line_count * step_count
    capacity = 2 * row_count // station_count
    total_steps = step_count * time_devices
    line_total = line_count * lax.axis_size("tile")
    station_gain = 1.0 / math.sqrt(line_total * total_steps / (station_count * tile_width))
    own_index = lax.axis_index("tm")

    own_cells = jnp.broadcast_to(model.astype(BF)[None], (device_count,) + model.shape)
    whole_model = swap(own_cells, AXES).reshape(-1, tile_width)

    partial_walk = running_sum(increments, False)
    offset = partial_walk + beyond(partial_walk[:, :, -1], False)[:, :, None] - observed
    positions = own_index * step_count + jnp.arange(step_count, dtype=jnp.int32)
    inside = (positions[None, :] < line_length[:, None]).reshape(row_count)

    flat_station = station_of.reshape(row_count)
    tile_of_row = flat_station // tile_width
    label = jnp.where(inside, flat_station % tile_width + 1, 0).astype(BF)
    block = 256
    tile_hot = (tile_of_row[:, None] == jnp.arange(station_count)).astype(BF)
    blocks = tile_hot.reshape(row_count // block, block, station_count)
    order = jnp.arange(block)
    before = (order[:, None] > order[None, :]).astype(BF)
    earlier_here = jnp.einsum("ij,bjt->bit", before, blocks, preferred_element_type=F32)
    totals = jnp.sum(blocks.astype(F32), axis=1)
    block_order = jnp.arange(row_count // block)
    block_before = (block_order[:, None] > block_order[None, :]).astype(BF)
    earlier_blocks = jnp.einsum("ab,bt->at", block_before, totals.astype(BF), preferred_element_type=F32)
    rank = jnp.sum(jnp.where(blocks > 0, earlier_here + earlier_blocks[:, None, :], 0.0), axis=2)
    rank = rank.reshape(row_count).astype(jnp.int32)
    rank_hot = rank[None, :] == jnp.arange(capacity)[:, None]

    flat_offset = offset.reshape(components, row_count)
    hi, mid, low = parts(flat_offset)
    stacked = jnp.concatenate([label[None], hi, mid, low], axis=0)
    spread = jnp.where(rank_hot[None], stacked[:, None, :], jnp.zeros((), BF))
    placed = jnp.einsum("crs,st->tcr", spread, tile_hot, preferred_element_type=F32)
    n = components
    outgoing = jnp.concatenate(
        [placed[:, :1], placed[:, 1 : 1 + n] + placed[:, 1 + n : 1 + 2 * n] + placed[:, 1 + 2 * n :]], axis=1
    )
    outgoing = outgoing.reshape(device_count, tiles_here, (n + 1) * capacity)
    arrived = swap(outgoing, AXES).reshape(device_count, tiles_here, n + 1, capacity)
    arrived = jnp.transpose(arrived, (1, 2, 0, 3)).reshape(tiles_here, n + 1, device_count * capacity)
    tags, values = arrived[:, 0], arrived[:, 1:]

    chosen = whole_model[tile_index]
    predicted = jnp.einsum("skcij,skj->sci", kernel, chosen, preferred_element_type=F32)
    station_ids = jnp.arange(1, tile_width + 1, dtype=jnp.int32)
    matches = (tags.astype(jnp.int32)[:, None, :] == station_ids[:, None]).astype(BF)
    three = jnp.concatenate(parts(predicted), axis=1)
    picked = jnp.einsum("sci,sir->scr", three, matches, preferred_element_type=F32)
    picked = picked[:, :n] + picked[:, n : 2 * n] + picked[:, 2 * n :]
    answer = jnp.where(tags[:, None] > 0, picked + values, 0.0)
    three = jnp.concatenate(parts(answer), axis=1)
    sums = jnp.einsum("scr,sir->sci", three, matches, preferred_element_type=F32)
    station_sums = sums[:, :n] + sums[:, n : 2 * n] + sums[:, 2 * n :]
    station_half = (station_sums * station_gain).astype(BF)

    back = answer.astype(BF).reshape(tiles_here, n, device_count, capacity)
    back = jnp.transpose(back, (2, 0, 1, 3)).reshape(device_count, tiles_here, n * capacity)
    returned = swap(back, AXES).reshape(station_count, n, capacity)
    wide = jnp.einsum("tcr,st->crs", returned, tile_hot, preferred_element_type=F32)
    residual = jnp.sum(jnp.where(rank_hot[None], wide, 0.0), axis=1)

    contributions = jnp.einsum("skcij,sci->skj", kernel, station_half, preferred_element_type=F32)
    cell_total = model.shape[0] * device_count
    cell_hot = (jnp.arange(cell_total)[:, None] == tile_index.reshape(-1)[None, :]).astype(F32)
    local_grad = jnp.matmul(cell_hot, contributions.reshape(-1, tile_width), precision=lax.Precision.HIGHEST)
    terms = swap(local_grad.reshape((device_count,) + model.shape), AXES)
    grad_model = jnp.sum(terms, axis=0)

    residual_block = residual.reshape(components, line_count, step_count)
    partial_tail = running_sum(residual_block, True)
    remaining = beyond(partial_tail[:, :, 0], True)
    grad_increments = (partial_tail + remaining[:, :, None]) / math.sqrt(total_steps)
    return (grad_model, grad_increments)


def solution(mesh):
    in_specs = (
        P(None, "tile", "tm"),
        P(None, "tile", "tm"),
        P(("tm", "tile"), None),
        P(("tm", "tile"), None, None, None, None),
        P(("tm", "tile"), None),
        P("tile", "tm"),
        P("tile"),
    )
    out_specs = (P(("tm", "tile"), None), P(None, "tile", "tm"))
    return jax.shard_map(shards, mesh=mesh, in_specs=in_specs, out_specs=out_specs, check_vma=False)
```

time: 416 us -> 115 us (0.28)
  local copies, waits for them, and re-layouts: 155 us -> 14.3 us
  waiting for transfers between devices: 113 us -> 31.9 us
  blocking collectives: 79.2 us -> 0 us
  starting transfers between devices: 21.1 us -> 38.6 us
  between operations: 14.5 us -> 1.11 us
  other arithmetic: 12.3 us -> 5.56 us
  matrix products: 18.8 us -> 23 us
    unnamed x2 -> x0, waiting for transfers between devices: 105 us -> none
    gather x16 -> x0, local copies, waits for them, and re-layouts: 84 us -> none  [the longest x1 25.7 us: shards(): placed = jnp.arange(row_count, dtype=jnp.int32) - starts[sorted_tiles]]
    all_gather x3 -> x0, blocking collectives: 79.2 us -> none  [the longest x1 42.2 us: shards(): lax.all_gather(model.astype(jnp.bfloat16), ('tm', 'tile'), axis=0, tiled=...]
    scatter x3 -> x0, local copies, waits for them, and re-layouts: 43.8 us -> none  [the longest x1 15.5 us: shards(): labels = jnp.full((station_count * capacity,), tile_width, jnp.int32).at[...]
    all_to_all x3 -> x6, waiting for transfers between devices: 8.07 us -> 31.9 us  [swap(): return lax.all_to_all(x, axes, split_axis=0, concat_axis=0, tiled=True)]
    all_to_all x3 -> x6, starting transfers between devices: 20.8 us -> 38.6 us  [swap(): return lax.all_to_all(x, axes, split_axis=0, concat_axis=0, tiled=True)]
    unnamed x16, local copies, waits for them, and re-layouts: 13.8 us -> 1.94 us
    sort x1 -> x0, other arithmetic: 5.78 us -> none  [shards(): ordering = jnp.argsort(tile_of_row, stable=True)]
  transfers between devices with their start and end apart: 4 -> 6, of which waited for: 3 -> 6; matrix products, arithmetic and copies ran while one was open for 15% -> 24% of each run, Pallas kernels for 0% -> 0%
where the time goes in v1:
time: 115 us
  starting transfers between devices  38.6 us (34%)
  waiting for transfers between devices  31.9 us (28%)
  matrix products  23 us (20%)
  local copies, waits for them, and re-layouts  14.3 us (12%)
  other arithmetic  5.56 us (5%)
    all_to_all x6, starting transfers between devices, swap(): return lax.all_to_all(x, axes, split_axis=0, concat_axis=0, tiled=True)  38.6 us
    all_to_all x6, waiting for transfers between devices, swap(): return lax.all_to_all(x, axes, split_axis=0, concat_axis=0, tiled=True)  31.9 us
    dot_general x1, matrix products, shards(): jnp.einsum('skcij,skj->sci', kernel, chosen, preferred_element_type=F32)  6.2 us
    dot_general x1, matrix products, shards(): jnp.einsum('skcij,sci->skj', kernel, station_half, preferred_element_type...  5.01 us
    dot_general x1, matrix products, shards(): jnp.einsum('tcr,st->crs', returned, tile_hot, preferred_element_type=F32)  3.51 us
  transfers between devices with their start and end apart: 6, of which 6 were waited for; matrix products, arithmetic and copies ran while one was open for 24% of the time, Pallas kernels for 0%

profile of v1, /device:TPU:1, one launch (start us, length us, event | category | flops | bytes accessed | tf_op | source)
XLA Modules:
  0.0 114.5 jit_solution(4124204786546059927)
XLA Ops:
  0.6 0.9 copy-done
  1.5 0.3 convolution_bitcast_fusion
  1.9 0.1 slice.96
  2.0 0.3 copy.94
  2.3 0.1 broadcast_add_fusion
  2.5 0.1 copy.166
  2.6 0.1 copy.97
  2.8 0.6 broadcast_in_dim.120
  3.4 7.6 %all-to-all-start = ((f32[16,9,8]{1,2,0:T(8,128)}), f32[16,9,8]{1,2,0:T(8,128)S(1)}, u32[]{:S(2)}, u32[]{:S(2)}) async-start(f32[16,9,8]{1,2,0:T(8,128)} %broadcast_in_dim.120), calls=%async_computation | async-start | bytes 131072 | tf_op jit(solution)/shard_map/all_to_all | solution.py:44
  11.1 0.7 compare_bitcast_fusion.1
  11.8 0.7 reshape.252
  12.5 0.8 copy.128
  13.4 0.6 fusion.19
  14.0 0.1 fusion.64
  14.1 1.8 %fusion.7 = f32[16,256]{1,0:T(8,128)S(1)} fusion(f32[16,256]{1,0:T(8,128)S(1)} %fusion.64, s32[16,256]{1,0:T(8,128)S(1)} %add_select_fusion), kind=kOutput, calls=%fused_computation.10 | convolution fusion | flops 546369536 | bytes 49152 | tf_op jit(solution)/shard_map/ij,bjt->bit/dot_general | solution.py:86
  16.3 1.2 %all-to-all-done = f32[16,9,8]{1,2,0:T(8,128)S(1)} async-done(((f32[16,9,8]{1,2,0:T(8,128)}), f32[16,9,8]{1,2,0:T(8,128)S(1)}, u32[]{:S(2)}, u32[]{:S(2)}) %all-to-all-start) | async-done | bytes 4640 | tf_op jit(solution)/shard_map/all_to_all | solution.py:44
  17.5 0.8 broadcast_in_dim.126
  18.3 9.9 %all-to-all-start.2 = ((bf16[128,4,256]{2,1,0:T(4,128)(2,1)}), bf16[128,4,256]{2,1,0:T(4,128)(2,1)S(1)}, u32[]{:S(2)}, u32[]{:S(2)}) async-start(bf16[128,4,256]{2,1,0:T(4,128)(2,1)} %broadcast_in_dim.126), calls=%async_computation.2 | async-start | bytes 524288 | tf_op jit(solution)/shard_map/all_to_all | solution.py:44
  28.3 0.1 select_reduce_fusion.1
  28.4 0.1 copy.98
  28.4 0.1 add_subtract_fusion
  28.6 0.2 copy.129
  28.8 0.2 pad_maximum_fusion.2
  29.0 2.2 %fusion.4 = f32[256,28,32]{0,2,1:T(8,128)S(1)} fusion(pred[32,4096]{1,0:T(8,128)(4,1)S(1)} %iota_compare_fusion.5, bf16[28,4096]{1,0:T(8,128)(2,1)S(1)} %pad_maximum_fusion.2, s32[4096]{0:T(1024)S(1)} %add_select_fusion.1), kind=kOutput, calls=%fused_computation.5 | convolution fusion | flops 1883766784 | bytes 1294336 | tf_op jit(solution)/shard_map/crs,st->tcr/dot_general | solution.py:99
  31.3 1.3 %copy.99 = f32[256,10,32]{2,1,0:T(8,128)S(1)} copy(f32[256,10,32]{0,2,1:T(8,128)S(1)} %pad_maximum_fusion.1) | data formatting | bytes 655360 | tf_op jit(solution)/shard_map/concatenate | solution.py:101
  32.6 1.6 %reshape.257 = f32[128,2,320]{2,1,0:T(2,128)} reshape(f32[256,10,32]{2,1,0:T(8,128)S(1)} %copy.99) | data formatting | bytes 655360 | tf_op jit(solution)/shard_map/reshape | solution.py:104
  34.1 5.1 %all-to-all-done.2 = bf16[128,4,256]{2,1,0:T(4,128)(2,1)S(1)} async-done(((bf16[128,4,256]{2,1,0:T(4,128)(2,1)}), bf16[128,4,256]{2,1,0:T(4,128)(2,1)S(1)}, u32[]{:S(2)}, u32[]{:S(2)}) %all-to-all-start.2) | async-done | bytes 262176 | tf_op jit(solution)/shard_map/all_to_all | solution.py:44
  39.2 4.7 %all-to-all-start.1 = ((f32[128,2,320]{2,1,0:T(2,128)}), f32[128,2,320]{2,1,0:T(2,128)S(1)}, u32[]{:S(2)}, u32[]{:S(2)}) async-start(f32[128,2,320]{2,1,0:T(2,128)} %reshape.257), calls=%async_computation.1 | async-start | bytes 786432 | tf_op jit(solution)/shard_map/all_to_all | solution.py:44
  44.0 0.6 gather_fusion
  44.6 6.2 %convolution_bitcast_fusion.1 = f32[2,1,9,256,1]{3,1,4,2,0:T(1,128)S(1)} fusion(bf16[2,4,9,256,256]{4,3,2,1,0:T(8,128)(2,1)} %param.10, bf16[2,4,256,1,1]{2,3,1,4,0:T(2,128)(2,1)S(1)} %reshape.286), kind=kOutput, calls=%fused_computation.28 | convolution fusion | flops 9437184 | bytes 9459712 | tf_op jit(solution)/shard_map/skcij,skj->sci/dot_general | solution.py:110
  50.8 5.3 %all-to-all-done.1 = f32[128,2,320]{2,1,0:T(2,128)S(1)} async-done(((f32[128,2,320]{2,1,0:T(2,128)}), f32[128,2,320]{2,1,0:T(2,128)S(1)}, u32[]{:S(2)}, u32[]{:S(2)}) %all-to-all-start.1) | async-done | bytes 327712 | tf_op jit(solution)/shard_map/all_to_all | solution.py:44
  56.2 0.2 copy.100
  56.4 0.4 copy.101
  56.8 0.7 reshape.259
  57.5 1.5 %fusion.2 = f32[2,27,4096]{2,1,0:T(8,128)S(1)} fusion(s32[2,4096]{1,0:T(2,128)S(1)} %convert_bitcast_fusion, s32[256]{0:T(256)S(1)} %iota_add_fusion.1, bf16[2,9,256]{2,1,0:T(8,128)(2,1)S(1)} %get-tuple-element.16, bf16[2,9,256]{2,1,0:T(8,128)(2,1)S(1)} %get-tuple-element.15, bf16[2,9,256]{2,1,0:T(8,128)(2,1)S(1)} %bitcast.116), kind=kOutput, calls=%fused_computation.3 | convolution fusion | flops 115426304 | bytes 946176 | tf_op jit(solution)/shard_map/sci,sir->scr/dot_general | solution.py:114
  59.1 0.1 fusion.70
  59.2 0.7 fusion.68
  59.9 0.3 reshape.262
  60.2 0.2 copy.107
  60.4 0.8 copy.108
  61.3 4.7 %all-to-all-start.4 = ((bf16[128,2,288]{2,1,0:T(2,128)(2,1)}), bf16[128,2,288]{2,1,0:T(2,128)(2,1)S(1)}, u32[]{:S(2)}, u32[]{:S(2)}) async-start(bf16[128,2,288]{2,1,0:T(2,128)(2,1)} %copy.108), calls=%async_computation.4 | async-start | bytes 393216 | tf_op jit(solution)/shard_map/all_to_all | solution.py:44
  65.9 0.3 fusion.33
  66.2 0.6 pad_maximum_fusion
  66.8 1.6 %fusion = f32[2,27,256]{2,1,0:T(8,128)S(1)} fusion(s32[2,4096]{1,0:T(2,128)S(1)} %convert_bitcast_fusion, s32[256]{0:T(256)S(1)} %iota_add_fusion.1, bf16[2,27,4096]{2,0,1:T(2,128)(2,1)S(1)} %pad_maximum_fusion), kind=kOutput, calls=%fused_computation.1 | convolution fusion | flops 115343360 | bytes 531456 | tf_op jit(solution)/shard_map/scr,sir->sci/dot_general | solution.py:118
  68.5 5.0 %fusion.48 = f32[2,1,4,256,1]{3,1,4,2,0:T(1,128)S(1)} fusion(bf16[2,4,9,256,256]{4,3,2,1,0:T(8,128)(2,1)} %param.10, bf16[2,9,256,1,1]{2,1,0,3,4:T(8,128)(2,1)S(1)} %fusion.52), kind=kOutput, calls=%fused_computation.89 | convolution fusion | flops 9437184 | bytes 9454592 | tf_op jit(solution)/shard_map/skcij,sci->skj/dot_general | solution.py:128
  73.5 2.7 %all-to-all-done.4 = bf16[128,2,288]{2,1,0:T(2,128)(2,1)S(1)} async-done(((bf16[128,2,288]{2,1,0:T(2,128)(2,1)}), bf16[128,2,288]{2,1,0:T(2,128)(2,1)S(1)}, u32[]{:S(2)}, u32[]{:S(2)}) %all-to-all-start.4) | async-done | bytes 147488 | tf_op jit(solution)/shard_map/all_to_all | solution.py:44
  76.3 0.5 reshape.264
  76.7 3.5 %fusion.23 = f32[9,4096]{1,0:T(8,128)S(1)} fusion(s32[4096]{0:T(1024)S(1)} %add_select_fusion.1, pred[32,4096]{1,0:T(8,128)(4,1)S(1)} %iota_compare_fusion.5, bf16[256,9,32]{2,1,0:T(8,128)(2,1)S(1)} %reshape.264), kind=kOutput, calls=%fused_computation.26 | convolution fusion | flops 607350784 | bytes 442368 | tf_op jit(solution)/shard_map/tcr,st->crs/dot_general | solution.py:125
  80.2 0.1 reshape_reshape.3
  80.4 0.2 fusion.34
  80.6 0.3 copy.111
  80.9 0.1 copy.112
  81.0 0.1 add_bitcast_fusion
  81.1 0.1 copy.113
  81.3 0.6 broadcast_in_dim.133
  81.9 4.0 %all-to-all-start.5 = ((f32[16,9,8]{1,2,0:T(8,128)}), f32[16,9,8]{1,2,0:T(8,128)S(1)}, u32[]{:S(2)}, u32[]{:S(2)}) async-start(f32[16,9,8]{1,2,0:T(8,128)} %broadcast_in_dim.133), calls=%async_computation.5 | async-start | bytes 131072 | tf_op jit(solution)/shard_map/all_to_all | solution.py:44
  85.9 0.5 fusion.59
  86.4 1.1 copy.106
  87.6 4.9 %all-to-all-done.5 = f32[16,9,8]{1,2,0:T(8,128)S(1)} async-done(((f32[16,9,8]{1,2,0:T(8,128)}), f32[16,9,8]{1,2,0:T(8,128)S(1)}, u32[]{:S(2)}, u32[]{:S(2)}) %all-to-all-start.5) | async-done | bytes 4640 | tf_op jit(solution)/shard_map/all_to_all | solution.py:44
  92.5 7.6 %all-to-all-start.3 = ((f32[128,4,256]{2,1,0:T(4,128)}), f32[128,4,256]{2,1,0:T(4,128)S(1)}, u32[]{:S(2)}, u32[]{:S(2)}) async-start(f32[128,4,256]{2,1,0:T(4,128)} %copy.106), calls=%async_computation.3 | async-start | bytes 1048576 | tf_op jit(solution)/shard_map/all_to_all | solution.py:44
  100.1 0.1 select_reduce_fusion
  100.3 0.7 add_multiply_fusion
  101.0 12.7 %all-to-all-done.3 = f32[128,4,256]{2,1,0:T(4,128)S(1)} async-done(((f32[128,4,256]{2,1,0:T(4,128)}), f32[128,4,256]{2,1,0:T(4,128)S(1)}, u32[]{:S(2)}, u32[]{:S(2)}) %all-to-all-start.3) | async-done | bytes 524320 | tf_op jit(solution)/shard_map/all_to_all | solution.py:44
  113.8 0.7 reduce_sum.60
  (51 shorter events, 1.0 us)
Async XLA Ops:
  0.6 0.9 copy-start
  3.4 14.1 %all-to-all-start = ((f32[16,9,8]{1,2,0:T(8,128)}), f32[16,9,8]{1,2,0:T(8,128)S(1)}, u32[]{:S(2)}, u32[]{:S(2)}) async-start(f32[16,9,8]{1,2,0:T(8,128)} %broadcast_in_dim.120), calls=%async_computation | async-start | bytes 131072 | tf_op jit(solution)/shard_map/all_to_all | solution.py:44
  12.5 3.5 %copy-start.1 = (s32[8,512]{1,0:T(8,128)S(1)}, s32[8,512]{1,0:T(8,128)}, u32[]{:S(2)}) copy-start(s32[8,512]{1,0:T(8,128)} %param.12) | copy-start | bytes 49156
  14.0 2.1 %copy-start.4 = (s32[2,4]{1,0:T(2,128)S(1)}, s32[2,4]{1,0:T(2,128)}, u32[]{:S(2)}) copy-start(s32[2,4]{1,0:T(2,128)} %param.11) | copy-start | bytes 100
  14.1 2.2 %copy-start.3 = (f32[4,256]{1,0:T(4,128)S(1)}, f32[4,256]{1,0:T(4,128)}, u32[]{:S(2)}) copy-start(f32[4,256]{1,0:T(4,128)} %param.9) | copy-start | bytes 12292
  14.1 14.3 %copy-start.2 = (f32[9,8,512]{2,1,0:T(8,128)S(1)}, f32[9,8,512]{2,1,0:T(8,128)}, u32[]{:S(2)}) copy-start(f32[9,8,512]{2,1,0:T(8,128)} %param.7) | copy-start | bytes 442372
  18.3 20.9 %all-to-all-start.2 = ((bf16[128,4,256]{2,1,0:T(4,128)(2,1)}), bf16[128,4,256]{2,1,0:T(4,128)(2,1)S(1)}, u32[]{:S(2)}, u32[]{:S(2)}) async-start(bf16[128,4,256]{2,1,0:T(4,128)(2,1)} %broadcast_in_dim.126), calls=%async_computation.2 | async-start | bytes 524288 | tf_op jit(solution)/shard_map/all_to_all | solution.py:44
  39.2 17.0 %all-to-all-start.1 = ((f32[128,2,320]{2,1,0:T(2,128)}), f32[128,2,320]{2,1,0:T(2,128)S(1)}, u32[]{:S(2)}, u32[]{:S(2)}) async-start(f32[128,2,320]{2,1,0:T(2,128)} %reshape.257), calls=%async_computation.1 | async-start | bytes 786432 | tf_op jit(solution)/shard_map/all_to_all | solution.py:44
  61.3 15.0 %all-to-all-start.4 = ((bf16[128,2,288]{2,1,0:T(2,128)(2,1)}), bf16[128,2,288]{2,1,0:T(2,128)(2,1)S(1)}, u32[]{:S(2)}, u32[]{:S(2)}) async-start(bf16[128,2,288]{2,1,0:T(2,128)(2,1)} %copy.108), calls=%async_computation.4 | async-start | bytes 393216 | tf_op jit(solution)/shard_map/all_to_all | solution.py:44
  81.9 10.5 %all-to-all-start.5 = ((f32[16,9,8]{1,2,0:T(8,128)}), f32[16,9,8]{1,2,0:T(8,128)S(1)}, u32[]{:S(2)}, u32[]{:S(2)}) async-start(f32[16,9,8]{1,2,0:T(8,128)} %broadcast_in_dim.133), calls=%async_computation.5 | async-start | bytes 131072 | tf_op jit(solution)/shard_map/all_to_all | solution.py:44
  92.5 21.3 %all-to-all-start.3 = ((f32[128,4,256]{2,1,0:T(4,128)}), f32[128,4,256]{2,1,0:T(4,128)S(1)}, u32[]{:S(2)}, u32[]{:S(2)}) async-start(f32[128,4,256]{2,1,0:T(4,128)} %copy.106), calls=%async_computation.3 | async-start | bytes 1048576 | tf_op jit(solution)/shard_map/all_to_all | solution.py:44

commit v2 on v1

v2 whole, which is shorter than its diff:
```python
import functools
import math

import jax
import jax.numpy as jnp
from jax import lax
from jax.experimental import pallas as pl
from jax.experimental.pallas import tpu as pltpu
from jax.sharding import PartitionSpec as P

MESH = pl.DeviceIdType.MESH
BF = jnp.bfloat16
F32 = jnp.float32
I32 = jnp.int32
TM = 16
TILE = 8
DEV = TM * TILE
CAP = 32
SLOT = 16
COMPS = 9
LINES = 8
STEPS = 512
WIDTH = 256
HALF = 128
NNZ = 4
PAIRS = 8
LABEL = 9
LINE = 10
SPARE = 12


def iota(shape, dim):
    return lax.broadcasted_iota(I32, shape, dim)


def nn(a, b):
    return lax.dot_general(a, b, (((1,), (0,)), ((), ())), preferred_element_type=F32)


def nt(a, b):
    return lax.dot_general(a, b, (((1,), (1,)), ((), ())), preferred_element_type=F32)


def split(x, count):
    pieces = []
    for _ in range(count):
        top = x.astype(BF).astype(F32)
        pieces.append(top)
        x = x - top
    return pieces


def ones(mask):
    return jnp.where(mask, 1.0, 0.0).astype(BF)


def spare_lane(line, comp):
    return (line * 4 + comp // 4) * SLOT + SPARE + comp % 4


def body(
    obs_ref, inc_ref, model_ref, kern_ref, index_ref, station_ref, length_ref,
    grad_ref, walk_ref,
    kern_v, hot_v, spread_v, rank_v, off_v, stage_v, table_v, early_v, cell_v, adj_v, wide_v, res_v, fold_v,
    mod_out, mod_in, out1, in1, out2, in2, out3, in3,
    kern_sem, local_sem, send_sem, recv_sem,
):
    tm, tile = lax.axis_index("tm"), lax.axis_index("tile")
    me = tm * TILE + tile
    tiles = [lax.rem(tile + k, TILE) for k in range(TILE)]

    barrier = pltpu.get_barrier_semaphore()

    def greet(row, columns):
        for t in columns:
            pl.semaphore_signal(barrier, inc=1, device_id=(row, t), device_id_type=MESH)

    greet(tm, tiles[1:])

    def greet_row(i, _):
        greet(lax.rem(tm + i, TM), tiles)
        return 0

    lax.fori_loop(1, TM, greet_row, 0)
    fetch = pltpu.make_async_copy(kern_ref, kern_v, kern_sem)
    fetch.start()

    def send_row(src_of, dst, slot, row, columns):
        for t in columns:
            pltpu.make_async_remote_copy(
                src_ref=src_of(row * TILE + t), dst_ref=dst.at[me],
                send_sem=send_sem.at[slot], recv_sem=recv_sem.at[slot],
                device_id=(row, t), device_id_type=MESH,
            ).start()

    def send_all(src_of, dst, slot):
        own = pltpu.make_async_copy(src_of(me), dst.at[me], local_sem.at[slot])
        own.start()
        send_row(src_of, dst, slot, tm, tiles[1:])

        def one(i, _):
            send_row(src_of, dst, slot, lax.rem(tm + i, TM), tiles)
            return 0

        lax.fori_loop(1, TM, one, 0)
        return own

    def all_arrived(dst, slot, own):
        own.wait()
        span = dst.at[pl.ds(0, DEV - 1)]
        pltpu.make_async_copy(span, span, recv_sem.at[slot]).wait()

    def all_sent(dst, slot):
        span = dst.at[pl.ds(0, DEV - 1)]
        pltpu.make_async_copy(span, span, send_sem.at[slot]).wait()

    cells = model_ref[...]
    mod_out[...] = jnp.concatenate([cells[:, :HALF], cells[:, HALF:]], axis=0).astype(BF)

    upto = ones(iota((WIDTH, WIDTH), 0) <= iota((WIDTH, WIDTH), 1))
    steps = inc_ref[...]
    rows = COMPS * LINES
    first = jnp.concatenate(split(steps[:, :WIDTH], 3), axis=0).astype(BF)
    second = jnp.concatenate(split(steps[:, WIDTH:], 3), axis=0).astype(BF)
    first, second = nn(first, upto), nn(second, upto)
    first = first[:rows] + first[rows : 2 * rows] + first[2 * rows :]
    second = second[:rows] + second[rows : 2 * rows] + second[2 * rows :]
    second = second + first[:, WIDTH - 1 :]
    totals = second[:, WIDTH - 1 :]
    first = first - obs_ref[:, :WIDTH]
    second = second - obs_ref[:, WIDTH:]
    for j, part in enumerate((first[:, :HALF], first[:, HALF:], second[:, :HALF], second[:, HALF:])):
        off_v[pl.ds(j * DEV, rows), :] = part
        off_v[pl.ds(j * DEV + rows, DEV - rows), :] = jnp.zeros((DEV - rows, HALF), F32)

    pl.semaphore_wait(barrier, DEV - 1)
    own_mod = send_all(lambda p: mod_out, mod_in, 0)

    def one_line(l, base):
        lanes = pl.ds(pl.multiple_of(l * STEPS, STEPS), STEPS)
        station = station_ref[pl.ds(l, 1), :]
        owner = station // WIDTH
        inner = station % WIDTH
        line_place = (owner % 2) * HALF + owner // 2
        hit = iota((WIDTH, STEPS), 0) == line_place
        hot = ones(hit)
        hot_v[:, lanes] = hot
        ranks = []
        for h in range(2):
            part = slice(h * WIDTH, (h + 1) * WIDTH)
            count = nn(hot[:, part], upto)
            ranks.append(jnp.sum(jnp.where(hit[:, part], count + base, 0.0), axis=0, keepdims=True))
            base = base + count[:, WIDTH - 1 :]
        rank = jnp.concatenate(ranks, axis=1) - 1.0
        rank_v[pl.ds(l, 1), :] = rank
        position = tm * STEPS + iota((1, STEPS), 1)
        label = jnp.where(position < length_ref[l], inner + 1, 0).astype(F32)
        comp = iota((SLOT, STEPS), 0)
        values = jnp.concatenate([off_v[pl.ds(j * DEV + l, SLOT, stride=LINES), :] for j in range(4)], axis=1)
        values = jnp.where(comp == LABEL, label, values)
        values = jnp.where(comp == LINE, l.astype(F32), values)
        for r in range(CAP):
            spread_v[pl.ds(r * SLOT, SLOT), lanes] = jnp.where(rank == float(r), values, 0.0).astype(BF)
        return base

    lax.fori_loop(0, LINES, one_line, jnp.zeros((WIDTH, 1), F32))

    placed = nt(hot_v[...], spread_v[...])
    row = iota((rows, CAP * SLOT), 0)
    at_spare = iota((rows, CAP * SLOT), 1) == spare_lane(row % LINES, row // LINES)
    for s, part in enumerate(split(totals, 2)):
        extra = jnp.sum(jnp.where(at_spare, part, 0.0), axis=0, keepdims=True)
        half = placed[s * HALF : (s + 1) * HALF] + extra
        for g in range(4):
            stage_v[pl.ds(s * 4 + g, DEV, stride=8), :] = half[:, g * HALF : (g + 1) * HALF]

    def pack(dst):
        dst[...] = stage_v[...].reshape(DEV, 8, HALF).astype(BF)

    def unpack(src):
        stage_v[...] = src[...].astype(F32).reshape(DEV * 8, HALF)

    pack(out1)
    own1 = send_all(lambda p: out1.at[p], in1, 1)

    fetch.wait()
    all_arrived(mod_in, 0, own_mod)
    pair_row = iota((SLOT, DEV * 8), 0)
    pair_lane = iota((SLOT, DEV * 8), 1)
    base_row = jnp.full((SLOT, DEV * 8), -8, I32)
    for q in range(PAIRS):
        cell = index_ref[q // NNZ, q % NNZ]
        base_row = jnp.where(pair_row == q, (cell // 4) * 8 + cell % 4, base_row)
    every = mod_in[...].reshape(DEV * 8, HALF)
    chosen = jnp.concatenate([nn(ones(pair_lane == base_row + 4 * h), every) for h in range(2)], axis=1)
    cell_v[...] = chosen
    comp_row = iota((SLOT, WIDTH), 0)
    predicted = []
    for s in range(2):

        def forward(k, total):
            vector = cell_v[pl.ds(s * NNZ + k, 1), :]
            for c in range(COMPS):
                left = jnp.where(comp_row == c, vector, 0.0).astype(BF)
                total = total + nt(left, kern_v[(s * NNZ + k) * COMPS + c])
            return total

        predicted.append(lax.fori_loop(0, NNZ, forward, jnp.zeros((SLOT, WIDTH), F32)))

    all_arrived(in1, 1, own1)
    unpack(in1)
    for s in range(2):
        for g in range(4):
            table_v[s, pl.ds(g * HALF, HALF), :] = stage_v[pl.ds(s * 4 + g, DEV, stride=8), :].T
    q_row = iota((DEV, CAP * SLOT), 0)
    pick = ones(
        (iota((DEV, CAP * SLOT), 1) == spare_lane(q_row // SLOT, q_row % SLOT)) & (q_row % SLOT < COMPS)
    )
    q_lane = iota((CAP * SLOT, DEV), 1)
    put = ones(
        (iota((CAP * SLOT, DEV), 0) == spare_lane(q_lane // SLOT, q_lane % SLOT)) & (q_lane % SLOT < COMPS)
    )
    source, target = iota((DEV, DEV), 0), iota((DEV, DEV), 1)
    same_lines = source % TILE == target % TILE
    before = ones(same_lines & (source // TILE < target // TILE))
    after = ones(same_lines & (source // TILE > target // TILE))
    early = jnp.zeros((DEV, DEV), F32)
    for s in range(2):
        part = nn(pick, table_v[s].astype(BF))
        early = early + nn(part.astype(BF), before)
    early_v[...] = early

    lane_count = 2 * HALF
    slot_row = iota((SLOT, lane_count), 0)
    station_row = iota((WIDTH, lane_count), 0)
    sums = []
    line_sums = [jnp.zeros((SLOT, HALF), F32) for _ in range(LINES)]
    for s in range(2):
        three = jnp.concatenate(split(predicted[s], 3), axis=0).astype(BF)

        def slots(i, carry):
            total = carry[0]
            lines = list(carry[1:])
            start = pl.multiple_of(i * 2 * SLOT, 2 * SLOT)
            got = jnp.concatenate(
                [table_v[s, pl.ds(start, SLOT), :], table_v[s, pl.ds(start + SLOT, SLOT), :]], axis=1
            )
            label = got[LABEL : LABEL + 1]
            line = got[LINE : LINE + 1]
            match = ones(station_row == label.astype(I32) - 1)
            picked = nn(three, match)
            picked = picked[:SLOT] + picked[SLOT : 2 * SLOT] + picked[2 * SLOT :]
            value = picked + got
            for l in range(LINES):
                walk = early_v[pl.ds(l * SLOT, SLOT), :]
                value = value + jnp.where(line == float(l), jnp.concatenate([walk, walk], axis=1), 0.0)
            value = jnp.where((label > 0.0) & (slot_row < COMPS), value, 0.0)
            res_v[s, pl.ds(start, SLOT), :] = value[:, :HALF]
            res_v[s, pl.ds(start + SLOT, SLOT), :] = value[:, HALF:]
            for l in range(LINES):
                mine = jnp.where(line == float(l), value, 0.0)
                lines[l] = lines[l] + mine[:, :HALF] + mine[:, HALF:]
            total = total + nt(jnp.concatenate(split(value, 3), axis=0).astype(BF), match)
            return (total, *lines)

        carry = lax.fori_loop(
            0, CAP // 2, slots, (jnp.zeros((3 * SLOT, WIDTH), F32), *line_sums)
        )
        sums.append(carry[0][:SLOT] + carry[0][SLOT : 2 * SLOT] + carry[0][2 * SLOT :])
        line_sums = list(carry[1:])

    gathered = jnp.concatenate(line_sums, axis=0)
    three = nn(jnp.concatenate(split(gathered, 3), axis=0).astype(BF), after)
    beyond = three[:DEV] + three[DEV : 2 * DEV] + three[2 * DEV :]
    for s, part in enumerate(split(beyond, 2)):
        full = res_v[s] + nn(put, part.astype(BF))
        for g in range(4):
            stage_v[pl.ds(s * 4 + g, DEV, stride=8), :] = full[g * HALF : (g + 1) * HALF, :].T
    pack(out2)
    own2 = send_all(lambda p: out2.at[p], in2, 2)

    gain = 1.0 / math.sqrt(LINES * TILE * STEPS * TM / (2 * DEV * WIDTH))
    for s in range(2):
        adj_v[s] = (sums[s] * gain).astype(BF).astype(F32)
    contributions = jnp.zeros((SLOT, WIDTH), F32)
    for s in range(2):

        def adjoint(k, total):
            for c in range(COMPS):
                left = jnp.where(comp_row == s * NNZ + k, adj_v[s, pl.ds(c, 1), :], 0.0).astype(BF)
                total = total + nn(left, kern_v[(s * NNZ + k) * COMPS + c])
            return total

        contributions = lax.fori_loop(0, NNZ, adjoint, contributions)
    pieces = [piece[:PAIRS] for piece in split(contributions, 2)]
    stack = [piece[:, h * HALF : (h + 1) * HALF] for h in range(2) for piece in pieces]
    stack = jnp.concatenate(stack + [jnp.zeros((HALF - 4 * PAIRS, HALF), F32)], axis=0).astype(BF)
    lane = iota((1, HALF), 1)
    goal = jnp.full((1, HALF), -8, I32)
    for q in range(PAIRS):
        cell = index_ref[q // NNZ, q % NNZ]
        goal = jnp.where(lane % PAIRS == q, (cell // 4) * 8 + cell % 4, goal)
    goal = jnp.where(lane < 4 * PAIRS, goal + 4 * (lane // (2 * PAIRS)), -8)
    stage_v[...] = nn(ones(iota((DEV * 8, HALF), 0) == goal), stack)
    pack(out3)
    own3 = send_all(lambda p: out3.at[p], in3, 3)

    all_arrived(in2, 2, own2)
    unpack(in2)
    for s in range(2):
        for g in range(4):
            wide_v[pl.ds(g * HALF, HALF), pl.ds(s * HALF, HALF)] = (
                stage_v[pl.ds(s * 4 + g, DEV, stride=8), :].T.astype(BF)
            )
    rest = jnp.sum(nn(pick, wide_v[...]), axis=1, keepdims=True)

    def collect(l, _):
        lanes = pl.ds(pl.multiple_of(l * STEPS, STEPS), STEPS)
        every = nn(wide_v[...], hot_v[:, lanes])
        rank = rank_v[pl.ds(l, 1), :]
        value = jnp.zeros((SLOT, STEPS), F32)
        for r in range(CAP):
            value = value + jnp.where(rank == float(r), every[r * SLOT : (r + 1) * SLOT], 0.0)
        fold_v[pl.ds(pl.multiple_of(l * SLOT, SLOT), SLOT), :] = value
        return 0

    lax.fori_loop(0, LINES, collect, 0)
    onward = ones(iota((WIDTH, WIDTH), 0) >= iota((WIDTH, WIDTH), 1))
    late = nn(fold_v[:, WIDTH:].astype(BF), onward) + rest
    soon = nn(fold_v[:, :WIDTH].astype(BF), onward) + late[:, :1]
    scale = 1.0 / math.sqrt(STEPS * TM)
    for j, part in enumerate((soon[:, :HALF], soon[:, HALF:], late[:, :HALF], late[:, HALF:])):
        for l in range(LINES):
            off_v[pl.ds(j * DEV + l, SLOT, stride=LINES), :] = part[l * SLOT : (l + 1) * SLOT] * scale
        walk_ref[:, pl.ds(j * HALF, HALF)] = off_v[pl.ds(j * DEV, rows), :]

    all_arrived(in3, 3, own3)
    grad = jnp.sum(in3[...].astype(F32), axis=0)
    grad_ref[...] = jnp.concatenate([grad[:4], grad[4:]], axis=1)
    for slot, dst in enumerate((mod_in, in1, in2, in3)):
        all_sent(dst, slot)


def shards(observed, increments, model, kernel, tile_index, station_of, line_length):
    rows = COMPS * LINES
    vmem = pl.BlockSpec(memory_space=pltpu.VMEM)
    smem = pl.BlockSpec(memory_space=pltpu.SMEM)
    message = pltpu.VMEM((DEV, 8, HALF), BF)
    grad_model, walk = pl.pallas_call(
        body,
        out_shape=(
            jax.ShapeDtypeStruct((4, WIDTH), F32),
            jax.ShapeDtypeStruct((rows, STEPS), F32),
        ),
        in_specs=[vmem, vmem, vmem, pl.BlockSpec(memory_space=pl.ANY), smem, vmem, smem],
        out_specs=(vmem, vmem),
        scratch_shapes=[
            pltpu.VMEM((PAIRS * COMPS, WIDTH, WIDTH), BF),
            pltpu.VMEM((WIDTH, LINES * STEPS), BF),
            pltpu.VMEM((CAP * SLOT, LINES * STEPS), BF),
            pltpu.VMEM((LINES, STEPS), F32),
            pltpu.VMEM((4 * DEV, HALF), F32),
            pltpu.VMEM((DEV * 8, HALF), F32),
            pltpu.VMEM((2, CAP * SLOT, HALF), F32),
            pltpu.VMEM((DEV, DEV), F32),
            pltpu.VMEM((SLOT, WIDTH), F32),
            pltpu.VMEM((2, SLOT, WIDTH), F32),
            pltpu.VMEM((CAP * SLOT, WIDTH), BF),
            pltpu.VMEM((2, CAP * SLOT, HALF), F32),
            pltpu.VMEM((DEV, STEPS), F32),
            pltpu.VMEM((8, HALF), BF),
            message, message, message, message, message, message, message,
            pltpu.SemaphoreType.DMA,
            pltpu.SemaphoreType.DMA((4,)),
            pltpu.SemaphoreType.DMA((4,)),
            pltpu.SemaphoreType.DMA((4,)),
        ],
        compiler_params=pltpu.CompilerParams(
            collective_id=0, has_side_effects=True, vmem_limit_bytes=48 * 1024 * 1024
        ),
        name="invert",
    )(
        observed.reshape(rows, STEPS),
        increments.reshape(rows, STEPS),
        model,
        kernel.reshape(PAIRS * COMPS, WIDTH, WIDTH),
        tile_index,
        station_of,
        line_length,
    )
    return grad_model, walk.reshape(COMPS, LINES, STEPS)


def solution(mesh):
    in_specs = (
        P(None, "tile", "tm"),
        P(None, "tile", "tm"),
        P(("tm", "tile"), None),
        P(("tm", "tile"), None, None, None, None),
        P(("tm", "tile"), None),
        P("tile", "tm"),
        P("tile"),
    )
    out_specs = (P(("tm", "tile"), None), P(None, "tile", "tm"))
    return jax.shard_map(shards, mesh=mesh, in_specs=in_specs, out_specs=out_specs, check_vma=False)
```

time: 115 us -> 54.3 us (0.47)
  Pallas kernels: 0 us -> 47.6 us
  starting transfers between devices: 38.6 us -> 0 us
  waiting for transfers between devices: 31.9 us -> 0 us
  matrix products: 23 us -> 0 us
  local copies, waits for them, and re-layouts: 14.3 us -> 5.8 us
  other arithmetic: 5.56 us -> 0 us
    pallas_call x0 -> x1, Pallas kernels: none -> 47.6 us  [shards(): pl.pallas_call(body, out_shape=(jax.ShapeDtypeStruct((4, WIDTH), F32), ja...]
    all_to_all x6 -> x0, starting transfers between devices: 38.6 us -> none  [swap(): return lax.all_to_all(x, axes, split_axis=0, concat_axis=0, tiled=True)]
    all_to_all x6 -> x0, waiting for transfers between devices: 31.9 us -> none  [swap(): return lax.all_to_all(x, axes, split_axis=0, concat_axis=0, tiled=True)]
    dot_general x11 -> x0, matrix products: 23 us -> none  [the longest x1 6.2 us: shards(): jnp.einsum('skcij,skj->sci', kernel, chosen, preferred_element_type=F32)]
    reshape x8 -> x0, local copies, waits for them, and re-layouts: 4.65 us -> none  [the longest x1 1.56 us: shards(): outgoing = outgoing.reshape(device_count, tiles_here, (n + 1) * capacity)]
    unnamed x16 -> x14, local copies, waits for them, and re-layouts: 1.94 us -> 5.8 us
    broadcast_in_dim x4 -> x0, local copies, waits for them, and re-layouts: 2.14 us -> none  [the longest x2 1.28 us: beyond(): everyone = swap(jnp.broadcast_to(part[None], (count,) + part.shape), 'tm')]
    reduce_sum x4 -> x0, other arithmetic: 1.54 us -> none  [the longest x1 0.74 us: shards(): grad_model = jnp.sum(terms, axis=0)]
  transfers between devices with their start and end apart: 6 -> 0, of which waited for: 6 -> 0; matrix products, arithmetic and copies ran while one was open for 24% -> 0% of each run, Pallas kernels for 0% -> 0%
where the time goes in v2:
time: 54.3 us; the launch traced here: 54 us
  Pallas kernels  47.6 us (88%)
  local copies, waits for them, and re-layouts  5.8 us (11%)
  between operations  0.65 us (1%)
    pallas_call x1, Pallas kernels, shards(): pl.pallas_call(body, out_shape=(jax.ShapeDtypeStruct((4, WIDTH), F32), ja...  47.6 us
    unnamed x14, local copies, waits for them, and re-layouts  5.8 us

profile of v2, /device:TPU:1, one launch (start us, length us, event | category | flops | bytes accessed | tf_op | source)
XLA Modules:
  0.0 54.0 jit_solution(14770263459954919678)
XLA Ops:
  0.6 0.0 copy-start
  0.6 0.9 %copy-done = f32[9,8,512]{2,1,0:T(8,128)S(1)} copy-done((f32[9,8,512]{2,1,0:T(8,128)S(1)}, f32[9,8,512]{2,1,0:T(8,128)}, u32[]{:S(2)}) %copy-start) | copy-done | bytes 147480
  1.5 0.0 copy-start.1
  1.5 0.9 %copy-done.1 = f32[9,8,512]{2,1,0:T(8,128)S(1)} copy-done((f32[9,8,512]{2,1,0:T(8,128)S(1)}, f32[9,8,512]{2,1,0:T(8,128)}, u32[]{:S(2)}) %copy-start.1) | copy-done | bytes 147480
  2.5 0.0 copy-start.2
  2.5 0.7 %copy-done.2 = s32[8,512]{1,0:T(8,128)S(1)} copy-done((s32[8,512]{1,0:T(8,128)S(1)}, s32[8,512]{1,0:T(8,128)}, u32[]{:S(2)}) %copy-start.2) | copy-done | bytes 16408
  3.2 0.0 copy-start.3
  3.2 0.7 %copy-done.3 = f32[4,256]{1,0:T(4,128)S(1)} copy-done((f32[4,256]{1,0:T(4,128)S(1)}, f32[4,256]{1,0:T(4,128)}, u32[]{:S(2)}) %copy-start.3) | copy-done | bytes 4120
  3.9 0.0 copy-start.4
  3.9 0.7 %copy-done.4 = s32[2,4]{1,0:T(2,128)S(1)} copy-done((s32[2,4]{1,0:T(2,128)S(1)}, s32[2,4]{1,0:T(2,128)}, u32[]{:S(2)}) %copy-start.4) | copy-done | bytes 56
  4.5 0.0 copy-start.5
  4.5 0.7 %copy-done.5 = s32[8]{0:T(128)S(1)} copy-done((s32[8]{0:T(128)S(1)}, s32[8]{0:T(128)}, u32[]{:S(2)}) %copy-start.5) | copy-done | bytes 56
  5.2 47.6 %invert.1 = (f32[4,256]{1,0:T(4,128)S(1)}, f32[72,512]{1,0:T(8,128)S(1)}) custom-call(f32[72,512]{1,0:T(8,128)S(1)} %bitcast.5, f32[72,512]{1,0:T(8,128)S(1)} %bitcast.6, f32[4,256]{1,0:T(4,128)S(1)} %copy-done.3, bf16[72,256,256]{2,1,0:T(8,128)(2,1)} %bitcast.7, s32[2,4]{1,0:T(2,128)S(1)} %copy-done.4, s32[8,512]{1,0:T(8,128)S(1)} %copy-done.2, s32[8]{0:T(128)S(1)} %copy-done.5), custom_call_target="tpu_custom_call" | custom-call | tf_op jit(solution)/shard_map/invert/pallas_call | solution.py:349
  52.8 0.6 %copy.11 = f32[4,256]{1,0:T(4,128)} copy(f32[4,256]{1,0:T(4,128)S(1)} %get-tuple-element.8) | data formatting | bytes 8192
  53.4 0.7 %copy.12 = f32[9,8,512]{2,1,0:T(8,128)} copy(f32[9,8,512]{2,1,0:T(8,128)S(1)} %bitcast.4) | data formatting | bytes 294912
Async XLA Ops:
  0.6 0.9 %copy-start = (f32[9,8,512]{2,1,0:T(8,128)S(1)}, f32[9,8,512]{2,1,0:T(8,128)}, u32[]{:S(2)}) copy-start(f32[9,8,512]{2,1,0:T(8,128)} %param.7) | copy-start | bytes 442372
  1.5 0.9 %copy-start.1 = (f32[9,8,512]{2,1,0:T(8,128)S(1)}, f32[9,8,512]{2,1,0:T(8,128)}, u32[]{:S(2)}) copy-start(f32[9,8,512]{2,1,0:T(8,128)} %param.8) | copy-start | bytes 442372
  2.5 0.7 %copy-start.2 = (s32[8,512]{1,0:T(8,128)S(1)}, s32[8,512]{1,0:T(8,128)}, u32[]{:S(2)}) copy-start(s32[8,512]{1,0:T(8,128)} %station_ref.1) | copy-start | bytes 49156
  3.2 0.7 %copy-start.3 = (f32[4,256]{1,0:T(4,128)S(1)}, f32[4,256]{1,0:T(4,128)}, u32[]{:S(2)}) copy-start(f32[4,256]{1,0:T(4,128)} %model_ref.1) | copy-start | bytes 12292
  3.9 0.7 %copy-start.4 = (s32[2,4]{1,0:T(2,128)S(1)}, s32[2,4]{1,0:T(2,128)}, u32[]{:S(2)}) copy-start(s32[2,4]{1,0:T(2,128)} %index_ref.1) | copy-start | bytes 100
  4.5 0.7 %copy-start.5 = (s32[8]{0:T(128)S(1)}, s32[8]{0:T(128)}, u32[]{:S(2)}) copy-start(s32[8]{0:T(128)} %length_ref.1) | copy-start | bytes 100

commit v3 on v2

--- a/solution.py
+++ b/solution.py
@@ -18,6 +18,7 @@
 CAP = 32
 SLOT = 16
 COMPS = 9
+CHUNK = 64
 LINES = 8
 STEPS = 512
 WIDTH = 256
@@ -27,6 +28,8 @@
 LABEL = 9
 LINE = 10
 SPARE = 12
+GRID = sorted(((x, y) for x in range(4) for y in range(4)), key=lambda o: -sum(min(v, 4 - v) for v in o))
+COLUMNS = (4, 5, 3, 2, 6, 7, 1, 0)
 
 
 def iota(shape, dim):
@@ -59,23 +62,35 @@
 
 
 def body(
-    obs_ref, inc_ref, model_ref, kern_ref, index_ref, station_ref, length_ref,
+    obs_hbm, inc_hbm, model_hbm, kern_ref, index_hbm, station_hbm, length_hbm,
     grad_ref, walk_ref,
-    kern_v, hot_v, spread_v, rank_v, off_v, stage_v, table_v, early_v, cell_v, adj_v, wide_v, res_v, fold_v,
+    obs_ref, inc_ref, model_ref, index_ref, station_ref, length_ref,
+    kern_v, hot_v, spread_v, rank_v, off_v, stage_v, table_v, early_v, cell_v, pred_v, adj_v, wide_v, res_v, fold_v,
     mod_out, mod_in, out1, in1, out2, in2, out3, in3,
-    kern_sem, local_sem, send_sem, recv_sem,
+    load_sem, kern_sem, local_sem, send_sem, recv_sem,
 ):
     tm, tile = lax.axis_index("tm"), lax.axis_index("tile")
     me = tm * TILE + tile
-    tiles = [lax.rem(tile + k, TILE) for k in range(TILE)]
-
+    tiles = [lax.rem(tile + k, TILE) for k in COLUMNS]
+
+    loads = [
+        pltpu.make_async_copy(hbm, ref, load_sem.at[i])
+        for i, (hbm, ref) in enumerate(
+            (
+                (inc_hbm, inc_ref), (obs_hbm, obs_ref), (model_hbm, model_ref),
+                (station_hbm, station_ref), (length_hbm, length_ref), (index_hbm, index_ref),
+            )
+        )
+    ]
+    for load in loads:
+        load.start()
     barrier = pltpu.get_barrier_semaphore()
 
     def greet(row, columns):
         for t in columns:
             pl.semaphore_signal(barrier, inc=1, device_id=(row, t), device_id_type=MESH)
 
-    greet(tm, tiles[1:])
+    greet(tm, tiles[:-1])
 
     def greet_row(i, _):
         greet(lax.rem(tm + i, TM), tiles)
@@ -85,24 +100,18 @@
     fetch = pltpu.make_async_copy(kern_ref, kern_v, kern_sem)
     fetch.start()
 
-    def send_row(src_of, dst, slot, row, columns):
-        for t in columns:
-            pltpu.make_async_remote_copy(
-                src_ref=src_of(row * TILE + t), dst_ref=dst.at[me],
-                send_sem=send_sem.at[slot], recv_sem=recv_sem.at[slot],
-                device_id=(row, t), device_id_type=MESH,
-            ).start()
-
     def send_all(src_of, dst, slot):
         own = pltpu.make_async_copy(src_of(me), dst.at[me], local_sem.at[slot])
         own.start()
-        send_row(src_of, dst, slot, tm, tiles[1:])
-
-        def one(i, _):
-            send_row(src_of, dst, slot, lax.rem(tm + i, TM), tiles)
-            return 0
-
-        lax.fori_loop(1, TM, one, 0)
+        for dx, dy in GRID:
+            row = lax.rem(tm // 4 + dx, 4) * 4 + lax.rem(lax.rem(tm, 4) + dy, 4)
+            for k, t in zip(COLUMNS, tiles):
+                if (dx, dy, k) != (0, 0, 0):
+                    pltpu.make_async_remote_copy(
+                        src_ref=src_of(row * TILE + t), dst_ref=dst.at[me],
+                        send_sem=send_sem.at[slot], recv_sem=recv_sem.at[slot],
+                        device_id=(row, t), device_id_type=MESH,
+                    ).start()
         return own
 
     def all_arrived(dst, slot, own):
@@ -114,6 +123,8 @@
         span = dst.at[pl.ds(0, DEV - 1)]
         pltpu.make_async_copy(span, span, send_sem.at[slot]).wait()
 
+    for load in loads:
+        load.wait()
     cells = model_ref[...]
     mod_out[...] = jnp.concatenate([cells[:, :HALF], cells[:, HALF:]], axis=0).astype(BF)
 
@@ -132,9 +143,6 @@
     for j, part in enumerate((first[:, :HALF], first[:, HALF:], second[:, :HALF], second[:, HALF:])):
         off_v[pl.ds(j * DEV, rows), :] = part
         off_v[pl.ds(j * DEV + rows, DEV - rows), :] = jnp.zeros((DEV - rows, HALF), F32)
-
-    pl.semaphore_wait(barrier, DEV - 1)
-    own_mod = send_all(lambda p: mod_out, mod_in, 0)
 
     def one_line(l, base):
         lanes = pl.ds(pl.multiple_of(l * STEPS, STEPS), STEPS)
@@ -181,6 +189,8 @@
         stage_v[...] = src[...].astype(F32).reshape(DEV * 8, HALF)
 
     pack(out1)
+    pl.semaphore_wait(barrier, DEV - 1)
+    own_mod = send_all(lambda p: mod_out, mod_in, 0)
     own1 = send_all(lambda p: out1.at[p], in1, 1)
 
     fetch.wait()
@@ -194,18 +204,27 @@
     every = mod_in[...].reshape(DEV * 8, HALF)
     chosen = jnp.concatenate([nn(ones(pair_lane == base_row + 4 * h), every) for h in range(2)], axis=1)
     cell_v[...] = chosen
-    comp_row = iota((SLOT, WIDTH), 0)
-    predicted = []
-    for s in range(2):
-
-        def forward(k, total):
-            vector = cell_v[pl.ds(s * NNZ + k, 1), :]
-            for c in range(COMPS):
-                left = jnp.where(comp_row == c, vector, 0.0).astype(BF)
-                total = total + nt(left, kern_v[(s * NNZ + k) * COMPS + c])
-            return total
-
-        predicted.append(lax.fori_loop(0, NNZ, forward, jnp.zeros((SLOT, WIDTH), F32)))
+    comp_row = iota((SLOT, HALF), 0)
+    for s in range(2):
+        vectors = [cell_v[pl.ds(s * NNZ + k, 1), :] for k in range(NNZ)]
+
+        def forward(c, halves):
+            sums = []
+            for i in range(0, WIDTH, CHUNK):
+                total = jnp.zeros((CHUNK, HALF), F32)
+                for k in range(NNZ):
+                    block = kern_v[(s * NNZ + k) * COMPS + c, pl.ds(i, CHUNK), :].astype(F32) * vectors[k]
+                    total = total + block[:, :HALF] + block[:, HALF:]
+                sums.append(total)
+            rows_here = []
+            for h in range(2):
+                tall = jnp.concatenate(sums[h * HALF // CHUNK : (h + 1) * HALF // CHUNK], axis=0).T
+                rows_here.append(jnp.where(comp_row == c, jnp.sum(tall, axis=0, keepdims=True), halves[h]))
+            return tuple(rows_here)
+
+        halves = lax.fori_loop(0, COMPS, forward, (jnp.zeros((SLOT, HALF), F32),) * 2)
+        for h in range(2):
+            pred_v[s, :, pl.ds(h * HALF, HALF)] = halves[h]
 
     all_arrived(in1, 1, own1)
     unpack(in1)
@@ -233,24 +252,26 @@
     lane_count = 2 * HALF
     slot_row = iota((SLOT, lane_count), 0)
     station_row = iota((WIDTH, lane_count), 0)
-    sums = []
-    line_sums = [jnp.zeros((SLOT, HALF), F32) for _ in range(LINES)]
-    for s in range(2):
-        three = jnp.concatenate(split(predicted[s], 3), axis=0).astype(BF)
-
-        def slots(i, carry):
-            total = carry[0]
-            lines = list(carry[1:])
-            start = pl.multiple_of(i * 2 * SLOT, 2 * SLOT)
-            got = jnp.concatenate(
-                [table_v[s, pl.ds(start, SLOT), :], table_v[s, pl.ds(start + SLOT, SLOT), :]], axis=1
-            )
+    tables = [[pred_v[s, :, pl.ds(h * HALF, HALF)] for h in range(2)] for s in range(2)]
+
+    def slots(i, carry):
+        totals = list(carry[:2])
+        lines = list(carry[2:])
+        start = pl.multiple_of(i * 2 * SLOT, 2 * SLOT)
+        for s in range(2):
+            pair = [table_v[s, pl.ds(start + j * SLOT, SLOT), :] for j in range(2)]
+            got = jnp.concatenate(pair, axis=1)
             label = got[LABEL : LABEL + 1]
             line = got[LINE : LINE + 1]
             match = ones(station_row == label.astype(I32) - 1)
-            picked = nn(three, match)
-            picked = picked[:SLOT] + picked[SLOT : 2 * SLOT] + picked[2 * SLOT :]
-            value = picked + got
+            picked = []
+            for part in pair:
+                at = jnp.broadcast_to(jnp.maximum(part[LABEL : LABEL + 1].astype(I32) - 1, 0), (SLOT, HALF))
+                lane = at % HALF
+                low = jnp.take_along_axis(tables[s][0], lane, axis=1)
+                high = jnp.take_along_axis(tables[s][1], lane, axis=1)
+                picked.append(jnp.where(at >= HALF, high, low))
+            value = jnp.concatenate(picked, axis=1) + got
             for l in range(LINES):
                 walk = early_v[pl.ds(l * SLOT, SLOT), :]
                 value = value + jnp.where(line == float(l), jnp.concatenate([walk, walk], axis=1), 0.0)
@@ -260,14 +281,15 @@
             for l in range(LINES):
                 mine = jnp.where(line == float(l), value, 0.0)
                 lines[l] = lines[l] + mine[:, :HALF] + mine[:, HALF:]
-            total = total + nt(jnp.concatenate(split(value, 3), axis=0).astype(BF), match)
-            return (total, *lines)
-
-        carry = lax.fori_loop(
-            0, CAP // 2, slots, (jnp.zeros((3 * SLOT, WIDTH), F32), *line_sums)
-        )
-        sums.append(carry[0][:SLOT] + carry[0][SLOT : 2 * SLOT] + carry[0][2 * SLOT :])
-        line_sums = list(carry[1:])
+            totals[s] = totals[s] + nt(jnp.concatenate(split(value, 3), axis=0).astype(BF), match)
+        return (*totals, *lines)
+
+    carry = lax.fori_loop(
+        0, CAP // 2, slots,
+        (*[jnp.zeros((3 * SLOT, WIDTH), F32)] * 2, *[jnp.zeros((SLOT, HALF), F32)] * LINES),
+    )
+    sums = [total[:SLOT] + total[SLOT : 2 * SLOT] + total[2 * SLOT :] for total in carry[:2]]
+    line_sums = list(carry[2:])
 
     gathered = jnp.concatenate(line_sums, axis=0)
     three = nn(jnp.concatenate(split(gathered, 3), axis=0).astype(BF), after)
@@ -280,19 +302,28 @@
     own2 = send_all(lambda p: out2.at[p], in2, 2)
 
     gain = 1.0 / math.sqrt(LINES * TILE * STEPS * TM / (2 * DEV * WIDTH))
-    for s in range(2):
-        adj_v[s] = (sums[s] * gain).astype(BF).astype(F32)
-    contributions = jnp.zeros((SLOT, WIDTH), F32)
-    for s in range(2):
-
-        def adjoint(k, total):
+    filler = jnp.zeros((HALF - SLOT, WIDTH), F32)
+    for s in range(2):
+        sheet = jnp.concatenate([(sums[s] * gain).astype(BF).astype(F32), filler], axis=0)
+        adj_v[s] = jnp.concatenate([sheet[:, :HALF].T, sheet[:, HALF:].T], axis=0)
+    contributions = []
+    for s in range(2):
+
+        def adjoint(i, totals):
+            totals = list(totals)
+            start = pl.multiple_of(i * CHUNK, CHUNK)
+            weights = adj_v[s, pl.ds(start, CHUNK), :]
             for c in range(COMPS):
-                left = jnp.where(comp_row == s * NNZ + k, adj_v[s, pl.ds(c, 1), :], 0.0).astype(BF)
-                total = total + nn(left, kern_v[(s * NNZ + k) * COMPS + c])
-            return total
-
-        contributions = lax.fori_loop(0, NNZ, adjoint, contributions)
-    pieces = [piece[:PAIRS] for piece in split(contributions, 2)]
+                weight = jnp.broadcast_to(weights[:, c : c + 1], (CHUNK, WIDTH))
+                for k in range(NNZ):
+                    block = kern_v[(s * NNZ + k) * COMPS + c, pl.ds(start, CHUNK), :].astype(F32) * weight
+                    totals[k] = totals[k] + jnp.sum(block.reshape(CHUNK // 8, 8, WIDTH), axis=0)
+            return tuple(totals)
+
+        totals = lax.fori_loop(0, WIDTH // CHUNK, adjoint, (jnp.zeros((8, WIDTH), F32),) * NNZ)
+        contributions += [jnp.sum(total, axis=0, keepdims=True) for total in totals]
+    contributions = jnp.concatenate(contributions, axis=0)
+    pieces = split(contributions, 2)
     stack = [piece[:, h * HALF : (h + 1) * HALF] for h in range(2) for piece in pieces]
     stack = jnp.concatenate(stack + [jnp.zeros((HALF - 4 * PAIRS, HALF), F32)], axis=0).astype(BF)
     lane = iota((1, HALF), 1)
@@ -344,7 +375,6 @@
 def shards(observed, increments, model, kernel, tile_index, station_of, line_length):
     rows = COMPS * LINES
     vmem = pl.BlockSpec(memory_space=pltpu.VMEM)
-    smem = pl.BlockSpec(memory_space=pltpu.SMEM)
     message = pltpu.VMEM((DEV, 8, HALF), BF)
     grad_model, walk = pl.pallas_call(
         body,
@@ -352,9 +382,15 @@
             jax.ShapeDtypeStruct((4, WIDTH), F32),
             jax.ShapeDtypeStruct((rows, STEPS), F32),
         ),
-        in_specs=[vmem, vmem, vmem, pl.BlockSpec(memory_space=pl.ANY), smem, vmem, smem],
+        in_specs=[pl.BlockSpec(memory_space=pl.ANY)] * 7,
         out_specs=(vmem, vmem),
         scratch_shapes=[
+            pltpu.VMEM((rows, STEPS), F32),
+            pltpu.VMEM((rows, STEPS), F32),
+            pltpu.VMEM((4, WIDTH), F32),
+            pltpu.SMEM((2, NNZ), I32),
+            pltpu.VMEM((LINES, STEPS), I32),
+            pltpu.SMEM((LINES,), I32),
             pltpu.VMEM((PAIRS * COMPS, WIDTH, WIDTH), BF),
             pltpu.VMEM((WIDTH, LINES * STEPS), BF),
             pltpu.VMEM((CAP * SLOT, LINES * STEPS), BF),
@@ -365,18 +401,20 @@
             pltpu.VMEM((DEV, DEV), F32),
             pltpu.VMEM((SLOT, WIDTH), F32),
             pltpu.VMEM((2, SLOT, WIDTH), F32),
+            pltpu.VMEM((2, WIDTH, HALF), F32),
             pltpu.VMEM((CAP * SLOT, WIDTH), BF),
             pltpu.VMEM((2, CAP * SLOT, HALF), F32),
             pltpu.VMEM((DEV, STEPS), F32),
             pltpu.VMEM((8, HALF), BF),
             message, message, message, message, message, message, message,
+            pltpu.SemaphoreType.DMA((6,)),
             pltpu.SemaphoreType.DMA,
             pltpu.SemaphoreType.DMA((4,)),
             pltpu.SemaphoreType.DMA((4,)),
             pltpu.SemaphoreType.DMA((4,)),
         ],
         compiler_params=pltpu.CompilerParams(
-            collective_id=0, has_side_effects=True, vmem_limit_bytes=48 * 1024 * 1024
+            collective_id=0, has_side_effects=True, vmem_limit_bytes=60 * 1024 * 1024
         ),
         name="invert",
     )(

time: 54.3 us -> 43.5 us (0.80)
  Pallas kernels: 47.6 us -> 39.9 us
  local copies, waits for them, and re-layouts: 5.8 us -> 2.84 us
    pallas_call x1, Pallas kernels: 47.6 us -> 39.9 us  [shards(): pl.pallas_call(body, out_shape=(jax.ShapeDtypeStruct((4, WIDTH), F32), ja...]
    unnamed x14 -> x2, local copies, waits for them, and re-layouts: 5.8 us -> 2.84 us
where the time goes in v3:
time: 43.5 us; the launch traced here: 43.4 us
  Pallas kernels  39.9 us (92%)
  local copies, waits for them, and re-layouts  2.84 us (7%)
  between operations  0.64 us (1%)
    pallas_call x1, Pallas kernels, shards(): pl.pallas_call(body, out_shape=(jax.ShapeDtypeStruct((4, WIDTH), F32), ja...  39.9 us
    unnamed x2, local copies, waits for them, and re-layouts  2.84 us

profile of v3, /device:TPU:1, one launch (start us, length us, event | category | flops | bytes accessed | tf_op | source)
XLA Modules:
  0.0 43.4 jit_solution(10106984765295010078)
XLA Ops:
  0.6 39.9 %invert.1 = (f32[4,256]{1,0:T(4,128)}, f32[72,512]{1,0:T(8,128)}) custom-call(f32[72,512]{1,0:T(8,128)} %bitcast.6, f32[72,512]{1,0:T(8,128)} %bitcast.7, f32[4,256]{1,0:T(4,128)} %model_hbm.1, bf16[72,256,256]{2,1,0:T(8,128)(2,1)} %bitcast.4, s32[2,4]{1,0:T(2,128)} %index_hbm.1, s32[8,512]{1,0:T(8,128)} %station_hbm.1, s32[8]{0:T(128)} %length_hbm.1), custom_call_target="tpu_custom_call" | custom-call | tf_op jit(solution)/shard_map/invert/pallas_call | solution.py:379
  40.5 1.3 %copy.11 = f32[4,256]{1,0:T(4,128)} copy(f32[4,256]{1,0:T(4,128)} %get-tuple-element.8) | data formatting | bytes 8192
  41.8 1.6 %copy.12 = f32[9,8,512]{2,1,0:T(8,128)} copy(f32[9,8,512]{2,1,0:T(8,128)} %bitcast.5) | data formatting | bytes 294912

commit v4 on v3

--- a/solution.py
+++ b/solution.py
@@ -19,6 +19,7 @@
 SLOT = 16
 COMPS = 9
 CHUNK = 64
+LANE_COMPS = 6
 LINES = 8
 STEPS = 512
 WIDTH = 256
@@ -63,11 +64,11 @@
 
 def body(
     obs_hbm, inc_hbm, model_hbm, kern_ref, index_hbm, station_hbm, length_hbm,
-    grad_ref, walk_ref,
-    obs_ref, inc_ref, model_ref, index_ref, station_ref, length_ref,
+    grad_hbm, walk_hbm,
+    grad_ref, obs_ref, inc_ref, model_ref, index_ref, station_ref, length_ref,
     kern_v, hot_v, spread_v, rank_v, off_v, stage_v, table_v, early_v, cell_v, pred_v, adj_v, wide_v, res_v, fold_v,
     mod_out, mod_in, out1, in1, out2, in2, out3, in3,
-    load_sem, kern_sem, local_sem, send_sem, recv_sem,
+    load_sem, save_sem, kern_sem, local_sem, send_sem, recv_sem,
 ):
     tm, tile = lax.axis_index("tm"), lax.axis_index("tile")
     me = tm * TILE + tile
@@ -205,26 +206,35 @@
     chosen = jnp.concatenate([nn(ones(pair_lane == base_row + 4 * h), every) for h in range(2)], axis=1)
     cell_v[...] = chosen
     comp_row = iota((SLOT, HALF), 0)
+    wide_row = iota((SLOT, WIDTH), 0)
     for s in range(2):
         vectors = [cell_v[pl.ds(s * NNZ + k, 1), :] for k in range(NNZ)]
 
-        def forward(c, halves):
-            sums = []
-            for i in range(0, WIDTH, CHUNK):
-                total = jnp.zeros((CHUNK, HALF), F32)
-                for k in range(NNZ):
-                    block = kern_v[(s * NNZ + k) * COMPS + c, pl.ds(i, CHUNK), :].astype(F32) * vectors[k]
-                    total = total + block[:, :HALF] + block[:, HALF:]
-                sums.append(total)
-            rows_here = []
-            for h in range(2):
-                tall = jnp.concatenate(sums[h * HALF // CHUNK : (h + 1) * HALF // CHUNK], axis=0).T
-                rows_here.append(jnp.where(comp_row == c, jnp.sum(tall, axis=0, keepdims=True), halves[h]))
-            return tuple(rows_here)
-
-        halves = lax.fori_loop(0, COMPS, forward, (jnp.zeros((SLOT, HALF), F32),) * 2)
+        def forward(i, state):
+            halves, across = list(state[:2]), state[2]
+            last = LANE_COMPS + i
+            for c in (2 * i, 2 * i + 1):
+                sums = []
+                for j in range(0, WIDTH, CHUNK):
+                    total = jnp.zeros((CHUNK, HALF), F32)
+                    for k in range(NNZ):
+                        block = kern_v[(s * NNZ + k) * COMPS + c, pl.ds(j, CHUNK), :].astype(F32) * vectors[k]
+                        total = total + block[:, :HALF] + block[:, HALF:]
+                    sums.append(total)
+                for h in range(2):
+                    tall = jnp.concatenate(sums[h * HALF // CHUNK : (h + 1) * HALF // CHUNK], axis=0).T
+                    halves[h] = jnp.where(comp_row == c, jnp.sum(tall, axis=0, keepdims=True), halves[h])
+            for k in range(NNZ):
+                left = jnp.where(wide_row == last, vectors[k], 0.0).astype(BF)
+                across = across + nt(left, kern_v[(s * NNZ + k) * COMPS + last])
+            return (*halves, across)
+
+        state = lax.fori_loop(
+            0, LANE_COMPS // 2, forward, (*[jnp.zeros((SLOT, HALF), F32)] * 2, jnp.zeros((SLOT, WIDTH), F32))
+        )
         for h in range(2):
-            pred_v[s, :, pl.ds(h * HALF, HALF)] = halves[h]
+            part = slice(h * HALF, (h + 1) * HALF)
+            pred_v[s, :, pl.ds(h * HALF, HALF)] = state[h] + state[2][:, part]
 
     all_arrived(in1, 1, own1)
     unpack(in1)
@@ -303,26 +313,31 @@
 
     gain = 1.0 / math.sqrt(LINES * TILE * STEPS * TM / (2 * DEV * WIDTH))
     filler = jnp.zeros((HALF - SLOT, WIDTH), F32)
+    contributions = []
+    across = jnp.zeros((SLOT, WIDTH), F32)
     for s in range(2):
-        sheet = jnp.concatenate([(sums[s] * gain).astype(BF).astype(F32), filler], axis=0)
-        adj_v[s] = jnp.concatenate([sheet[:, :HALF].T, sheet[:, HALF:].T], axis=0)
-    contributions = []
-    for s in range(2):
-
-        def adjoint(i, totals):
-            totals = list(totals)
+        sheet = (sums[s] * gain).astype(BF).astype(F32)
+        tall = jnp.concatenate([sheet, filler], axis=0)
+        adj_v[s] = jnp.concatenate([tall[:, :HALF].T, tall[:, HALF:].T], axis=0)
+
+        def adjoint(i, state):
+            totals, across = list(state[:NNZ]), state[NNZ]
             start = pl.multiple_of(i * CHUNK, CHUNK)
             weights = adj_v[s, pl.ds(start, CHUNK), :]
-            for c in range(COMPS):
+            for c in range(LANE_COMPS):
                 weight = jnp.broadcast_to(weights[:, c : c + 1], (CHUNK, WIDTH))
                 for k in range(NNZ):
                     block = kern_v[(s * NNZ + k) * COMPS + c, pl.ds(start, CHUNK), :].astype(F32) * weight
                     totals[k] = totals[k] + jnp.sum(block.reshape(CHUNK // 8, 8, WIDTH), axis=0)
-            return tuple(totals)
-
-        totals = lax.fori_loop(0, WIDTH // CHUNK, adjoint, (jnp.zeros((8, WIDTH), F32),) * NNZ)
-        contributions += [jnp.sum(total, axis=0, keepdims=True) for total in totals]
-    contributions = jnp.concatenate(contributions, axis=0)
+            for c in range(LANE_COMPS, COMPS):
+                left = jnp.where(wide_row == s * NNZ + i, sheet[c : c + 1], 0.0).astype(BF)
+                across = across + nn(left, kern_v[(s * NNZ + i) * COMPS + c])
+            return (*totals, across)
+
+        state = lax.fori_loop(0, NNZ, adjoint, (*[jnp.zeros((8, WIDTH), F32)] * NNZ, across))
+        contributions += [jnp.sum(total, axis=0, keepdims=True) for total in state[:NNZ]]
+        across = state[NNZ]
+    contributions = jnp.concatenate(contributions, axis=0) + across[:PAIRS]
     pieces = split(contributions, 2)
     stack = [piece[:, h * HALF : (h + 1) * HALF] for h in range(2) for piece in pieces]
     stack = jnp.concatenate(stack + [jnp.zeros((HALF - 4 * PAIRS, HALF), F32)], axis=0).astype(BF)
@@ -360,21 +375,35 @@
     late = nn(fold_v[:, WIDTH:].astype(BF), onward) + rest
     soon = nn(fold_v[:, :WIDTH].astype(BF), onward) + late[:, :1]
     scale = 1.0 / math.sqrt(STEPS * TM)
+    saves = []
     for j, part in enumerate((soon[:, :HALF], soon[:, HALF:], late[:, :HALF], late[:, HALF:])):
         for l in range(LINES):
             off_v[pl.ds(j * DEV + l, SLOT, stride=LINES), :] = part[l * SLOT : (l + 1) * SLOT] * scale
-        walk_ref[:, pl.ds(j * HALF, HALF)] = off_v[pl.ds(j * DEV, rows), :]
+        save = pltpu.make_async_copy(
+            off_v.at[pl.ds(j * DEV, rows)], walk_hbm.at[:, pl.ds(j * HALF, HALF)], save_sem.at[j]
+        )
+        save.start()
+        saves.append(save)
 
     all_arrived(in3, 3, own3)
     grad = jnp.sum(in3[...].astype(F32), axis=0)
     grad_ref[...] = jnp.concatenate([grad[:4], grad[4:]], axis=1)
+    save = pltpu.make_async_copy(grad_ref, grad_hbm, save_sem.at[4])
+    save.start()
+    for save in saves + [save]:
+        save.wait()
     for slot, dst in enumerate((mod_in, in1, in2, in3)):
         all_sent(dst, slot)
 
 
+def deliver(grad_in, walk_in, grad_out, walk_out):
+    walk_out[...] = walk_in[...]
+    grad_out[...] = grad_in[...]
+
+
 def shards(observed, increments, model, kernel, tile_index, station_of, line_length):
     rows = COMPS * LINES
-    vmem = pl.BlockSpec(memory_space=pltpu.VMEM)
+    anywhere = pl.BlockSpec(memory_space=pl.ANY)
     message = pltpu.VMEM((DEV, 8, HALF), BF)
     grad_model, walk = pl.pallas_call(
         body,
@@ -382,9 +411,10 @@
             jax.ShapeDtypeStruct((4, WIDTH), F32),
             jax.ShapeDtypeStruct((rows, STEPS), F32),
         ),
-        in_specs=[pl.BlockSpec(memory_space=pl.ANY)] * 7,
-        out_specs=(vmem, vmem),
+        in_specs=[anywhere] * 7,
+        out_specs=(anywhere, anywhere),
         scratch_shapes=[
+            pltpu.VMEM((4, WIDTH), F32),
             pltpu.VMEM((rows, STEPS), F32),
             pltpu.VMEM((rows, STEPS), F32),
             pltpu.VMEM((4, WIDTH), F32),
@@ -408,6 +438,7 @@
             pltpu.VMEM((8, HALF), BF),
             message, message, message, message, message, message, message,
             pltpu.SemaphoreType.DMA((6,)),
+            pltpu.SemaphoreType.DMA((5,)),
             pltpu.SemaphoreType.DMA,
             pltpu.SemaphoreType.DMA((4,)),
             pltpu.SemaphoreType.DMA((4,)),
@@ -426,6 +457,14 @@
         station_of,
         line_length,
     )
+    grad_model, walk = pl.pallas_call(
+        deliver,
+        out_shape=(
+            jax.ShapeDtypeStruct((4, WIDTH), F32),
+            jax.ShapeDtypeStruct((rows, STEPS), F32),
+        ),
+        name="deliver",
+    )(grad_model, walk)
     return grad_model, walk.reshape(COMPS, LINES, STEPS)
 
 

time: 43.5 us -> 40.7 us (0.936)
  local copies, waits for them, and re-layouts: 2.84 us -> 0 us
    unnamed x2 -> x0, local copies, waits for them, and re-layouts: 2.84 us -> none
    pallas_call x0 -> x1, Pallas kernels: none -> 1.59 us  [shards(): pl.pallas_call(deliver, out_shape=(jax.ShapeDtypeStruct((4, WIDTH), F32),...]
    pallas_call x1, Pallas kernels: 39.9 us -> 38.3 us  [shards(): pl.pallas_call(body, out_shape=(jax.ShapeDtypeStruct((4, WIDTH), F32), ja...]
where the time goes in v4:
time: 40.7 us; the launch traced here: 40.5 us
  Pallas kernels  39.9 us (98%)
  between operations  0.64 us (2%)
    pallas_call x1, Pallas kernels, shards(): pl.pallas_call(body, out_shape=(jax.ShapeDtypeStruct((4, WIDTH), F32), ja...  38.3 us
    pallas_call x1, Pallas kernels, shards(): pl.pallas_call(deliver, out_shape=(jax.ShapeDtypeStruct((4, WIDTH), F32),...  1.59 us

profile of v4, /device:TPU:1, one launch (start us, length us, event | category | flops | bytes accessed | tf_op | source)
XLA Modules:
  0.0 40.5 jit_solution(17237425047015442592)
XLA Ops:
  0.6 38.3 %invert.1 = (f32[4,256]{1,0:T(4,128)}, f32[72,512]{1,0:T(8,128)}) custom-call(f32[72,512]{1,0:T(8,128)} %bitcast.5, f32[72,512]{1,0:T(8,128)} %bitcast.6, f32[4,256]{1,0:T(4,128)} %model_hbm.1, bf16[72,256,256]{2,1,0:T(8,128)(2,1)} %bitcast.4, s32[2,4]{1,0:T(2,128)} %index_hbm.1, s32[8,512]{1,0:T(8,128)} %station_hbm.1, s32[8]{0:T(128)} %length_hbm.1), custom_call_target="tpu_custom_call" | custom-call | tf_op jit(solution)/shard_map/invert/pallas_call | solution.py:408
  39.0 1.6 %deliver.1 = (f32[4,256]{1,0:T(4,128)}, f32[72,512]{1,0:T(8,128)}) custom-call(f32[4,256]{1,0:T(4,128)} %get-tuple-element.6.grad_in, f32[72,512]{1,0:T(8,128)} %get-tuple-element.7.walk_in), custom_call_target="tpu_custom_call" | custom-call | tf_op jit(solution)/shard_map/deliver/pallas_call | solution.py:460

commit v5 on v4

--- a/solution.py
+++ b/solution.py
@@ -66,7 +66,7 @@
     obs_hbm, inc_hbm, model_hbm, kern_ref, index_hbm, station_hbm, length_hbm,
     grad_hbm, walk_hbm,
     grad_ref, obs_ref, inc_ref, model_ref, index_ref, station_ref, length_ref,
-    kern_v, hot_v, spread_v, rank_v, off_v, stage_v, table_v, early_v, cell_v, pred_v, adj_v, wide_v, res_v, fold_v,
+    kern_v, hot_v, spread_v, rank_v, off_v, pick_v, put_v, before_v, after_v, goal_v, onward_v, stage_v, placed_v, table_v, early_v, cell_v, pred_v, adj_v, wide_v, res_v, fold_v,
     mod_out, mod_in, out1, in1, out2, in2, out3, in3,
     load_sem, save_sem, kern_sem, local_sem, send_sem, recv_sem,
 ):
@@ -146,7 +146,7 @@
         off_v[pl.ds(j * DEV + rows, DEV - rows), :] = jnp.zeros((DEV - rows, HALF), F32)
 
     def one_line(l, base):
-        lanes = pl.ds(pl.multiple_of(l * STEPS, STEPS), STEPS)
+        lanes = pl.ds(l * STEPS, STEPS)
         station = station_ref[pl.ds(l, 1), :]
         owner = station // WIDTH
         inner = station % WIDTH
@@ -167,19 +167,27 @@
         comp = iota((SLOT, STEPS), 0)
         values = jnp.concatenate([off_v[pl.ds(j * DEV + l, SLOT, stride=LINES), :] for j in range(4)], axis=1)
         values = jnp.where(comp == LABEL, label, values)
-        values = jnp.where(comp == LINE, l.astype(F32), values)
+        values = jnp.where(comp == LINE, float(l), values)
         for r in range(CAP):
             spread_v[pl.ds(r * SLOT, SLOT), lanes] = jnp.where(rank == float(r), values, 0.0).astype(BF)
         return base
 
-    lax.fori_loop(0, LINES, one_line, jnp.zeros((WIDTH, 1), F32))
-
-    placed = nt(hot_v[...], spread_v[...])
+    def place(l):
+        lanes = pl.ds(l * STEPS, STEPS)
+        fresh = nt(hot_v[:, lanes], spread_v[:, lanes])
+        placed_v[...] = fresh if l == 0 else placed_v[...] + fresh
+
+    base = jnp.zeros((WIDTH, 1), F32)
+    for l in range(LINES):
+        base = one_line(l, base)
+        if l:
+            place(l - 1)
+    place(LINES - 1)
     row = iota((rows, CAP * SLOT), 0)
     at_spare = iota((rows, CAP * SLOT), 1) == spare_lane(row % LINES, row // LINES)
     for s, part in enumerate(split(totals, 2)):
         extra = jnp.sum(jnp.where(at_spare, part, 0.0), axis=0, keepdims=True)
-        half = placed[s * HALF : (s + 1) * HALF] + extra
+        half = placed_v[pl.ds(s * HALF, HALF), :] + extra
         for g in range(4):
             stage_v[pl.ds(s * 4 + g, DEV, stride=8), :] = half[:, g * HALF : (g + 1) * HALF]
 
@@ -194,6 +202,26 @@
     own_mod = send_all(lambda p: mod_out, mod_in, 0)
     own1 = send_all(lambda p: out1.at[p], in1, 1)
 
+    q_row = iota((DEV, CAP * SLOT), 0)
+    pick_v[...] = ones(
+        (iota((DEV, CAP * SLOT), 1) == spare_lane(q_row // SLOT, q_row % SLOT)) & (q_row % SLOT < COMPS)
+    )
+    q_lane = iota((CAP * SLOT, DEV), 1)
+    put_v[...] = ones(
+        (iota((CAP * SLOT, DEV), 0) == spare_lane(q_lane // SLOT, q_lane % SLOT)) & (q_lane % SLOT < COMPS)
+    )
+    source, target = iota((DEV, DEV), 0), iota((DEV, DEV), 1)
+    same_lines = source % TILE == target % TILE
+    before_v[...] = ones(same_lines & (source // TILE < target // TILE))
+    after_v[...] = ones(same_lines & (source // TILE > target // TILE))
+    lane = iota((1, HALF), 1)
+    goal = jnp.full((1, HALF), -8, I32)
+    for q in range(PAIRS):
+        cell = index_ref[q // NNZ, q % NNZ]
+        goal = jnp.where(lane % PAIRS == q, (cell // 4) * 8 + cell % 4, goal)
+    goal = jnp.where(lane < 4 * PAIRS, goal + 4 * (lane // (2 * PAIRS)), -8)
+    goal_v[...] = ones(iota((DEV * 8, HALF), 0) == goal)
+    onward_v[...] = ones(iota((WIDTH, WIDTH), 0) >= iota((WIDTH, WIDTH), 1))
     fetch.wait()
     all_arrived(mod_in, 0, own_mod)
     pair_row = iota((SLOT, DEV * 8), 0)
@@ -241,22 +269,10 @@
     for s in range(2):
         for g in range(4):
             table_v[s, pl.ds(g * HALF, HALF), :] = stage_v[pl.ds(s * 4 + g, DEV, stride=8), :].T
-    q_row = iota((DEV, CAP * SLOT), 0)
-    pick = ones(
-        (iota((DEV, CAP * SLOT), 1) == spare_lane(q_row // SLOT, q_row % SLOT)) & (q_row % SLOT < COMPS)
-    )
-    q_lane = iota((CAP * SLOT, DEV), 1)
-    put = ones(
-        (iota((CAP * SLOT, DEV), 0) == spare_lane(q_lane // SLOT, q_lane % SLOT)) & (q_lane % SLOT < COMPS)
-    )
-    source, target = iota((DEV, DEV), 0), iota((DEV, DEV), 1)
-    same_lines = source % TILE == target % TILE
-    before = ones(same_lines & (source // TILE < target // TILE))
-    after = ones(same_lines & (source // TILE > target // TILE))
     early = jnp.zeros((DEV, DEV), F32)
     for s in range(2):
-        part = nn(pick, table_v[s].astype(BF))
-        early = early + nn(part.astype(BF), before)
+        part = nn(pick_v[...], table_v[s].astype(BF))
+        early = early + nn(part.astype(BF), before_v[...])
     early_v[...] = early
 
     lane_count = 2 * HALF
@@ -295,17 +311,17 @@
         return (*totals, *lines)
 
     carry = lax.fori_loop(
-        0, CAP // 2, slots,
+        0, CAP // 2, slots, unroll=2, init_val=
         (*[jnp.zeros((3 * SLOT, WIDTH), F32)] * 2, *[jnp.zeros((SLOT, HALF), F32)] * LINES),
     )
     sums = [total[:SLOT] + total[SLOT : 2 * SLOT] + total[2 * SLOT :] for total in carry[:2]]
     line_sums = list(carry[2:])
 
     gathered = jnp.concatenate(line_sums, axis=0)
-    three = nn(jnp.concatenate(split(gathered, 3), axis=0).astype(BF), after)
+    three = nn(jnp.concatenate(split(gathered, 3), axis=0).astype(BF), after_v[...])
     beyond = three[:DEV] + three[DEV : 2 * DEV] + three[2 * DEV :]
     for s, part in enumerate(split(beyond, 2)):
-        full = res_v[s] + nn(put, part.astype(BF))
+        full = res_v[s] + nn(put_v[...], part.astype(BF))
         for g in range(4):
             stage_v[pl.ds(s * 4 + g, DEV, stride=8), :] = full[g * HALF : (g + 1) * HALF, :].T
     pack(out2)
@@ -334,20 +350,14 @@
                 across = across + nn(left, kern_v[(s * NNZ + i) * COMPS + c])
             return (*totals, across)
 
-        state = lax.fori_loop(0, NNZ, adjoint, (*[jnp.zeros((8, WIDTH), F32)] * NNZ, across))
+        state = lax.fori_loop(0, NNZ, adjoint, (*[jnp.zeros((8, WIDTH), F32)] * NNZ, across), unroll=2)
         contributions += [jnp.sum(total, axis=0, keepdims=True) for total in state[:NNZ]]
         across = state[NNZ]
     contributions = jnp.concatenate(contributions, axis=0) + across[:PAIRS]
     pieces = split(contributions, 2)
     stack = [piece[:, h * HALF : (h + 1) * HALF] for h in range(2) for piece in pieces]
     stack = jnp.concatenate(stack + [jnp.zeros((HALF - 4 * PAIRS, HALF), F32)], axis=0).astype(BF)
-    lane = iota((1, HALF), 1)
-    goal = jnp.full((1, HALF), -8, I32)
-    for q in range(PAIRS):
-        cell = index_ref[q // NNZ, q % NNZ]
-        goal = jnp.where(lane % PAIRS == q, (cell // 4) * 8 + cell % 4, goal)
-    goal = jnp.where(lane < 4 * PAIRS, goal + 4 * (lane // (2 * PAIRS)), -8)
-    stage_v[...] = nn(ones(iota((DEV * 8, HALF), 0) == goal), stack)
+    stage_v[...] = nn(goal_v[...], stack)
     pack(out3)
     own3 = send_all(lambda p: out3.at[p], in3, 3)
 
@@ -358,7 +368,7 @@
             wide_v[pl.ds(g * HALF, HALF), pl.ds(s * HALF, HALF)] = (
                 stage_v[pl.ds(s * 4 + g, DEV, stride=8), :].T.astype(BF)
             )
-    rest = jnp.sum(nn(pick, wide_v[...]), axis=1, keepdims=True)
+    rest = jnp.sum(nn(pick_v[...], wide_v[...]), axis=1, keepdims=True)
 
     def collect(l, _):
         lanes = pl.ds(pl.multiple_of(l * STEPS, STEPS), STEPS)
@@ -370,8 +380,8 @@
         fold_v[pl.ds(pl.multiple_of(l * SLOT, SLOT), SLOT), :] = value
         return 0
 
-    lax.fori_loop(0, LINES, collect, 0)
-    onward = ones(iota((WIDTH, WIDTH), 0) >= iota((WIDTH, WIDTH), 1))
+    lax.fori_loop(0, LINES, collect, 0, unroll=2)
+    onward = onward_v[...]
     late = nn(fold_v[:, WIDTH:].astype(BF), onward) + rest
     soon = nn(fold_v[:, :WIDTH].astype(BF), onward) + late[:, :1]
     scale = 1.0 / math.sqrt(STEPS * TM)
@@ -426,7 +436,14 @@
             pltpu.VMEM((CAP * SLOT, LINES * STEPS), BF),
             pltpu.VMEM((LINES, STEPS), F32),
             pltpu.VMEM((4 * DEV, HALF), F32),
+            pltpu.VMEM((DEV, CAP * SLOT), BF),
+            pltpu.VMEM((CAP * SLOT, DEV), BF),
+            pltpu.VMEM((DEV, DEV), BF),
+            pltpu.VMEM((DEV, DEV), BF),
+            pltpu.VMEM((DEV * 8, HALF), BF),
+            pltpu.VMEM((WIDTH, WIDTH), BF),
             pltpu.VMEM((DEV * 8, HALF), F32),
+            pltpu.VMEM((WIDTH, CAP * SLOT), F32),
             pltpu.VMEM((2, CAP * SLOT, HALF), F32),
             pltpu.VMEM((DEV, DEV), F32),
             pltpu.VMEM((SLOT, WIDTH), F32),

time: 40.7 us -> 37.9 us (0.931)
  Pallas kernels: 39.9 us -> 37.1 us
    pallas_call x1, Pallas kernels: 38.3 us -> 35.5 us  [shards(): pl.pallas_call(body, out_shape=(jax.ShapeDtypeStruct((4, WIDTH), F32), ja...]
where the time goes in v5:
time: 37.9 us; the launch traced here: 37.7 us
  Pallas kernels  37.1 us (98%)
  between operations  0.64 us (2%)
    pallas_call x1, Pallas kernels, shards(): pl.pallas_call(body, out_shape=(jax.ShapeDtypeStruct((4, WIDTH), F32), ja...  35.5 us
    pallas_call x1, Pallas kernels, shards(): pl.pallas_call(deliver, out_shape=(jax.ShapeDtypeStruct((4, WIDTH), F32),...  1.59 us

profile of v5, /device:TPU:1, one launch (start us, length us, event | category | flops | bytes accessed | tf_op | source)
XLA Modules:
  0.0 37.7 jit_solution(5314000062068660552)
XLA Ops:
  0.6 35.5 %invert.1 = (f32[4,256]{1,0:T(4,128)}, f32[72,512]{1,0:T(8,128)}) custom-call(f32[72,512]{1,0:T(8,128)} %bitcast.5, f32[72,512]{1,0:T(8,128)} %bitcast.6, f32[4,256]{1,0:T(4,128)} %model_hbm.1, bf16[72,256,256]{2,1,0:T(8,128)(2,1)} %bitcast.4, s32[2,4]{1,0:T(2,128)} %index_hbm.1, s32[8,512]{1,0:T(8,128)} %station_hbm.1, s32[8]{0:T(128)} %length_hbm.1), custom_call_target="tpu_custom_call" | custom-call | tf_op jit(solution)/shard_map/invert/pallas_call | solution.py:418
  36.1 1.6 %deliver.1 = (f32[4,256]{1,0:T(4,128)}, f32[72,512]{1,0:T(8,128)}) custom-call(f32[4,256]{1,0:T(4,128)} %get-tuple-element.6.grad_in, f32[72,512]{1,0:T(8,128)} %get-tuple-element.7.walk_in), custom_call_target="tpu_custom_call" | custom-call | tf_op jit(solution)/shard_map/deliver/pallas_call | solution.py:477

commit v6 on v5

--- a/solution.py
+++ b/solution.py
@@ -83,21 +83,15 @@
             )
         )
     ]
+    barrier = pltpu.get_barrier_semaphore()
+
+    for dx, dy in GRID:
+        row = lax.rem(tm // 4 + dx, 4) * 4 + lax.rem(lax.rem(tm, 4) + dy, 4)
+        for k, t in zip(COLUMNS, tiles):
+            if (dx, dy, k) != (0, 0, 0):
+                pl.semaphore_signal(barrier, inc=1, device_id=(row, t), device_id_type=MESH)
     for load in loads:
         load.start()
-    barrier = pltpu.get_barrier_semaphore()
-
-    def greet(row, columns):
-        for t in columns:
-            pl.semaphore_signal(barrier, inc=1, device_id=(row, t), device_id_type=MESH)
-
-    greet(tm, tiles[:-1])
-
-    def greet_row(i, _):
-        greet(lax.rem(tm + i, TM), tiles)
-        return 0
-
-    lax.fori_loop(1, TM, greet_row, 0)
     fetch = pltpu.make_async_copy(kern_ref, kern_v, kern_sem)
     fetch.start()
 
@@ -182,6 +176,9 @@
         base = one_line(l, base)
         if l:
             place(l - 1)
+        if l == 5:
+            pl.semaphore_wait(barrier, DEV - 1)
+            own_mod = send_all(lambda p: mod_out, mod_in, 0)
     place(LINES - 1)
     row = iota((rows, CAP * SLOT), 0)
     at_spare = iota((rows, CAP * SLOT), 1) == spare_lane(row % LINES, row // LINES)
@@ -198,8 +195,6 @@
         stage_v[...] = src[...].astype(F32).reshape(DEV * 8, HALF)
 
     pack(out1)
-    pl.semaphore_wait(barrier, DEV - 1)
-    own_mod = send_all(lambda p: mod_out, mod_in, 0)
     own1 = send_all(lambda p: out1.at[p], in1, 1)
 
     q_row = iota((DEV, CAP * SLOT), 0)
@@ -258,7 +253,7 @@
             return (*halves, across)
 
         state = lax.fori_loop(
-            0, LANE_COMPS // 2, forward, (*[jnp.zeros((SLOT, HALF), F32)] * 2, jnp.zeros((SLOT, WIDTH), F32))
+            0, LANE_COMPS // 2, forward, unroll=3, init_val=(*[jnp.zeros((SLOT, HALF), F32)] * 2, jnp.zeros((SLOT, WIDTH), F32))
         )
         for h in range(2):
             part = slice(h * HALF, (h + 1) * HALF)
@@ -311,7 +306,7 @@
         return (*totals, *lines)
 
     carry = lax.fori_loop(
-        0, CAP // 2, slots, unroll=2, init_val=
+        0, CAP // 2, slots, unroll=4, init_val=
         (*[jnp.zeros((3 * SLOT, WIDTH), F32)] * 2, *[jnp.zeros((SLOT, HALF), F32)] * LINES),
     )
     sums = [total[:SLOT] + total[SLOT : 2 * SLOT] + total[2 * SLOT :] for total in carry[:2]]
@@ -380,7 +375,7 @@
         fold_v[pl.ds(pl.multiple_of(l * SLOT, SLOT), SLOT), :] = value
         return 0
 
-    lax.fori_loop(0, LINES, collect, 0, unroll=2)
+    lax.fori_loop(0, LINES, collect, 0, unroll=4)
     onward = onward_v[...]
     late = nn(fold_v[:, WIDTH:].astype(BF), onward) + rest
     soon = nn(fold_v[:, :WIDTH].astype(BF), onward) + late[:, :1]

time: 37.9 us -> 36.5 us (0.963)
  Pallas kernels: 37.1 us -> 35.7 us
    pallas_call x1, Pallas kernels: 35.5 us -> 34.2 us  [shards(): pl.pallas_call(body, out_shape=(jax.ShapeDtypeStruct((4, WIDTH), F32), ja...]
where the time goes in v6:
time: 36.5 us; the launch traced here: 36.4 us
  Pallas kernels  35.7 us (98%)
  between operations  0.64 us (2%)
    pallas_call x1, Pallas kernels, shards(): pl.pallas_call(body, out_shape=(jax.ShapeDtypeStruct((4, WIDTH), F32), ja...  34.2 us
    pallas_call x1, Pallas kernels, shards(): pl.pallas_call(deliver, out_shape=(jax.ShapeDtypeStruct((4, WIDTH), F32),...  1.59 us

profile of v6, /device:TPU:1, one launch (start us, length us, event | category | flops | bytes accessed | tf_op | source)
XLA Modules:
  0.0 36.4 jit_solution(8968003276054325207)
XLA Ops:
  0.6 34.2 %invert.1 = (f32[4,256]{1,0:T(4,128)}, f32[72,512]{1,0:T(8,128)}) custom-call(f32[72,512]{1,0:T(8,128)} %bitcast.5, f32[72,512]{1,0:T(8,128)} %bitcast.6, f32[4,256]{1,0:T(4,128)} %model_hbm.1, bf16[72,256,256]{2,1,0:T(8,128)(2,1)} %bitcast.4, s32[2,4]{1,0:T(2,128)} %index_hbm.1, s32[8,512]{1,0:T(8,128)} %station_hbm.1, s32[8]{0:T(128)} %length_hbm.1), custom_call_target="tpu_custom_call" | custom-call | tf_op jit(solution)/shard_map/invert/pallas_call | solution.py:413
  34.8 1.6 %deliver.1 = (f32[4,256]{1,0:T(4,128)}, f32[72,512]{1,0:T(8,128)}) custom-call(f32[4,256]{1,0:T(4,128)} %get-tuple-element.6.grad_in, f32[72,512]{1,0:T(8,128)} %get-tuple-element.7.walk_in), custom_call_target="tpu_custom_call" | custom-call | tf_op jit(solution)/shard_map/deliver/pallas_call | solution.py:472

commit v7 on v6

--- a/solution.py
+++ b/solution.py
@@ -93,20 +93,23 @@
     for load in loads:
         load.start()
     fetch = pltpu.make_async_copy(kern_ref, kern_v, kern_sem)
-    fetch.start()
+
+    rows_of = {
+        (dx, dy): lax.rem(tm // 4 + dx, 4) * 4 + lax.rem(lax.rem(tm, 4) + dy, 4) for dx, dy in GRID
+    }
 
     def send_all(src_of, dst, slot):
         own = pltpu.make_async_copy(src_of(me), dst.at[me], local_sem.at[slot])
         own.start()
-        for dx, dy in GRID:
-            row = lax.rem(tm // 4 + dx, 4) * 4 + lax.rem(lax.rem(tm, 4) + dy, 4)
-            for k, t in zip(COLUMNS, tiles):
-                if (dx, dy, k) != (0, 0, 0):
-                    pltpu.make_async_remote_copy(
-                        src_ref=src_of(row * TILE + t), dst_ref=dst.at[me],
-                        send_sem=send_sem.at[slot], recv_sem=recv_sem.at[slot],
-                        device_id=(row, t), device_id_type=MESH,
-                    ).start()
+        for j in range(DEV):
+            (dx, dy), (k, t) = GRID[(5 * j + j // TM) % TM], (COLUMNS[j // TM], tiles[j // TM])
+            row = rows_of[dx, dy]
+            if (dx, dy, k) != (0, 0, 0):
+                pltpu.make_async_remote_copy(
+                    src_ref=src_of(row * TILE + t), dst_ref=dst.at[me],
+                    send_sem=send_sem.at[slot], recv_sem=recv_sem.at[slot],
+                    device_id=(row, t), device_id_type=MESH,
+                ).start()
         return own
 
     def all_arrived(dst, slot, own):
@@ -120,6 +123,7 @@
 
     for load in loads:
         load.wait()
+    fetch.start()
     cells = model_ref[...]
     mod_out[...] = jnp.concatenate([cells[:, :HALF], cells[:, HALF:]], axis=0).astype(BF)
 

time: 36.5 us -> 36.6 us (level)
  no operation moved by 1% of the time
where the time goes in v7:
time: 36.6 us; the launch traced here: 36.4 us
  Pallas kernels  35.8 us (98%)
  between operations  0.64 us (2%)
    pallas_call x1, Pallas kernels, shards(): pl.pallas_call(body, out_shape=(jax.ShapeDtypeStruct((4, WIDTH), F32), ja...  34.2 us
    pallas_call x1, Pallas kernels, shards(): pl.pallas_call(deliver, out_shape=(jax.ShapeDtypeStruct((4, WIDTH), F32),...  1.59 us

profile of v7, /device:TPU:1, one launch (start us, length us, event | category | flops | bytes accessed | tf_op | source)
XLA Modules:
  0.0 36.4 jit_solution(2056718892980952699)
XLA Ops:
  0.6 34.2 %invert.1 = (f32[4,256]{1,0:T(4,128)}, f32[72,512]{1,0:T(8,128)}) custom-call(f32[72,512]{1,0:T(8,128)} %bitcast.5, f32[72,512]{1,0:T(8,128)} %bitcast.6, f32[4,256]{1,0:T(4,128)} %model_hbm.1, bf16[72,256,256]{2,1,0:T(8,128)(2,1)} %bitcast.4, s32[2,4]{1,0:T(2,128)} %index_hbm.1, s32[8,512]{1,0:T(8,128)} %station_hbm.1, s32[8]{0:T(128)} %length_hbm.1), custom_call_target="tpu_custom_call" | custom-call | tf_op jit(solution)/shard_map/invert/pallas_call | solution.py:417
  34.8 1.6 %deliver.1 = (f32[4,256]{1,0:T(4,128)}, f32[72,512]{1,0:T(8,128)}) custom-call(f32[4,256]{1,0:T(4,128)} %get-tuple-element.6.grad_in, f32[72,512]{1,0:T(8,128)} %get-tuple-element.7.walk_in), custom_call_target="tpu_custom_call" | custom-call | tf_op jit(solution)/shard_map/deliver/pallas_call | solution.py:476
